TPU v7x, 32 devices: a whole 2x2x4 slice. The times are simulated.
32 devices in a mesh: groups: 2 (over y), ctx: 4 (over z), head: 2 (over x), pair: 2 (over core).
Axes of the slice: x: 2, y: 2, z: 4, core: 2. Of those that a mesh axis runs over, the one named last changes fastest.
Arguments:
- query_suffix: bfloat16 [3072, 40, 128], P(('groups', 'ctx'), ('head', 'pair')), parts along dimension 0, may hold values from -9 to 9
- key_suffix: bfloat16 [3072, 8, 128], P(('groups', 'ctx'), ('head', 'pair')), parts along dimension 0, may hold values from -4 to 4
- value_suffix: bfloat16 [3072, 8, 128], P(('groups', 'ctx'), ('head', 'pair')), parts along dimension 0, may hold values from -6 to 6
- key_prefix: bfloat16 [1024, 8, 128], P(('groups', 'ctx', 'pair'), 'head'), parts along dimension 0, may hold values from -4 to 4
- value_prefix: bfloat16 [1024, 8, 128], P(('groups', 'ctx', 'pair'), 'head'), parts along dimension 0, may hold values from -6 to 6
- file_ids: int32 [3072], P(('groups', 'ctx')), parts along dimension 0, may hold values from 0 to 3, never falling along the last dimension, each value on 1 to 768 neighbouring positions
Outputs:
- attention: bfloat16 [3072, 40, 128], P(('groups', 'ctx'), ('head', 'pair')), parts along dimension 0
There are 2 independent parts, one for each index of `groups`. A program takes and returns all parts, laid end to end along the dimension named above; each array names one. Nothing has to cross between parts.
Inputs may be any that keep to these rules, and one draw needn't show every extreme that they name: `file_ids`: file numbers never fall along the tokens; every file has 1 to 768 tokens, and one has exactly 768.
All inputs are finite; a program needn't handle non-finite values.
Results may differ from a plain program's by a relative error of at most 0.007.
Values may be sent and summed in bfloat16 or wider, within the bound.
No kernel may reach another device: no remote copies, remote signals or barrier semaphores. Data moves between devices by JAX's collectives and lax.ppermute only.
A program may use at most 64 MiB of HBM per device.

v0:
```python
import functools
import math

import jax
import jax.numpy as jnp
from jax import lax
from jax.experimental import pallas as pl
from jax.experimental.pallas import tpu as pltpu
from jax.sharding import PartitionSpec as P


HIDDEN = -1e30
TILE = 128
IDROWS = 16
CHUNK = 32
GRANT = 24 * 2**20
F32 = jnp.float32
BF16 = jnp.bfloat16
VM = pl.BlockSpec(memory_space=pltpu.VMEM)
HB = pl.BlockSpec(memory_space=pltpu.HBM)


def passed_on(value, hop):
    count = lax.axis_size("ctx")
    if hop == 1:
        pairs = [(i, (i + 1) % count) for i in range(count)]
    else:
        pairs = [(i, i + 1) for i in range(hop - 1, count - 1)]
    return lax.ppermute(value, "ctx", pairs)


def swapped(value, axis, bit):
    count = lax.axis_size(axis)
    return lax.ppermute(value, axis, [(i, i ^ bit) for i in range(count)])


def one_head_rows(src, first, rows, heads, wide, head):
    if head == 0:
        wide[0 : rows * heads, :] = src[first : first + rows * heads, :].astype(F32)
    return wide[pl.ds(head, rows, stride=heads), :]


def place_keys(src, rows, heads, wide, keys, at):
    for head in range(heads):
        picked = one_head_rows(src, 0, rows, heads, wide, head)
        for j in range(0, rows, TILE):
            keys[head, (at + j) // TILE] = jnp.transpose(picked[j : j + TILE, :]).astype(BF16)


def place_values(src, rows, heads, wide, vals, at):
    for head in range(heads):
        vals[head, at : at + rows, :] = one_head_rows(src, 0, rows, heads, wide, head).astype(BF16)


def id_column(ids, tile):
    return jnp.transpose(jnp.broadcast_to(ids[tile : tile + 1, :].astype(F32), (TILE, TILE)))


def id_row(ids, tile):
    return jnp.broadcast_to(ids[tile : tile + 1, :].astype(F32), (TILE, TILE))


def choose_kernel(kv_local, far_k, far_v, other_k, other_v, out, wide, own_k, own_v, sems):
    moves = [
        pltpu.make_async_copy(far_k, own_k, sems.at[0]),
        pltpu.make_async_copy(far_v, own_v, sems.at[1]),
    ]
    for move in moves:
        move.start()
    for move in moves:
        move.wait()
    positions = out.shape[0] // (4 * kv_local)
    heads = own_k.shape[0] // positions
    start = lax.axis_index("pair") * kv_local
    place = 0
    for mine, other in ((own_k, other_k), (own_v, other_v)):
        for slot, src in enumerate((mine, other)):
            wide[slot] = src[...].astype(F32)
        for head in range(kv_local):
            for slot in range(2):
                picked = wide[slot, pl.ds(start + head, positions, stride=heads), :]
                out[place : place + positions, :] = picked.astype(BF16)
                place += positions


def attend(q, keys, vals, masked, bias, factor, old, keep, emit, scores, peaks, tops, weights):
    qheads, rows, _ = q.shape
    blocks = keys.shape[1]
    group = qheads // keys.shape[0]

    def score(head, slot):
        kv = head // group
        wall = jnp.concatenate([keys[kv, j] for j in range(blocks)], axis=1)
        found = jnp.dot(q[head], wall, preferred_element_type=F32)
        peak = None
        for j in range(blocks):
            piece = found[:, j * TILE : (j + 1) * TILE]
            if j < masked:
                piece = piece + bias[j]
            scores[slot, j] = piece
            peak = piece if peak is None else jnp.maximum(peak, piece)
        peaks[slot] = peak

    def weigh(head, slot):
        for r in range(0, rows, CHUNK):
            part = slice(r, r + CHUNK)
            top = jnp.max(peaks[slot, part, :], axis=1, keepdims=True)
            top = jnp.broadcast_to(top, (CHUNK, TILE))
            if old is not None:
                top = jnp.maximum(top, old[head, part, :])
            if keep is None:
                tops[slot, part, :] = top
            else:
                keep[head, part, :] = top
            for j in range(blocks):
                shifted = (scores[slot, j, part, :] - top) * factor
                weights[slot, j, part, :] = jnp.exp2(shifted).astype(BF16)

    def mix(head, slot):
        wall = jnp.concatenate([weights[slot, j] for j in range(blocks)], axis=1)
        mine = vals[head // group]
        mine = jnp.concatenate([mine, jnp.ones_like(mine)], axis=1)
        mixed = jnp.dot(wall, mine, preferred_element_type=F32)
        emit(head, tops[slot] if keep is None else keep[head], mixed)

    def step(head, slot):
        score(head + 1, 1 - slot)
        weigh(head, slot)
        mix(head - 1, 1 - slot)

    score(0, 0)
    score(1, 1)
    weigh(0, 0)
    trips = (qheads - 2) // 2

    def trip(index, _):
        head = 1 + 2 * index
        step(head, 1)
        step(head + 1, 0)
        return 0

    lax.fori_loop(0, trips, trip, 0)
    for head in range(1 + 2 * trips, qheads - 1):
        step(head, head % 2)
    last = qheads - 1
    weigh(last, last % 2)
    mix(last - 1, (last - 1) % 2)
    mix(last, last % 2)


def absorb_kernel(plan, kv_local, rows, factor, *refs):
    refs = list(refs)
    q, ids = refs.pop(0), refs.pop(0)
    started, final = plan["old"], plan["final"]
    acc = refs.pop(0) if started else None
    stat = refs.pop(0) if started else None
    sources = [(kind, [refs.pop(0) for _ in range(taken)]) for kind, taken in plan["parts"]]
    outs = [refs.pop(0) for _ in range(1 if final else 2)]
    moves = []
    if not started:
        landed, k_here, v_here, sems = refs.pop(0), *refs[-3:]
        refs = refs[:-3]
        (kind, (k_far, v_far)) = sources[0]
        sources[0] = (kind, (k_here, v_here))
        moves = [
            pltpu.make_async_copy(k_far, k_here, sems.at[0]),
            pltpu.make_async_copy(v_far, v_here, sems.at[1]),
            pltpu.make_async_copy(q, landed, sems.at[2]),
        ]
        for move in moves:
            move.start()
        moves[0].wait()
        moves[1].wait()
        q = landed
    keys, vals, wide, bias, *room = refs
    tiles = rows // TILE
    mine = ids[...]
    at = 0
    masked = 0
    for kind, taken in sources:
        if kind == "prefix":
            size = 2 * kv_local * TILE
            for chunk in taken:
                for first in range(0, chunk.shape[0], size):
                    for head in range(kv_local):
                        low = first + head * TILE
                        keys[head, at // TILE] = jnp.transpose(chunk[low : low + TILE, :])
                        low = first + (kv_local + head) * TILE
                        vals[head, at : at + TILE, :] = chunk[low : low + TILE, :]
                    at += TILE
            continue
        place_keys(taken[0], rows, kv_local, wide, keys, at)
        place_values(taken[1], rows, kv_local, wide, vals, at)
        if kind == "own":
            other = mine
            spot = lax.broadcasted_iota(jnp.int32, (TILE, TILE), 0)
            place = lax.broadcasted_iota(jnp.int32, (TILE, TILE), 1)
        else:
            hops = 1 if kind == "back1" else 2
            other = taken[1][rows * kv_local : rows * kv_local + IDROWS, :].astype(F32)
            other = jnp.where(lax.axis_index("ctx") >= hops, other, 0.0)
        for i in range(tiles):
            column = id_column(mine, i)
            part = slice(i * TILE, (i + 1) * TILE)
            for j in range(tiles):
                seen = column == id_row(other, j)
                if kind == "own" and j == i:
                    seen = seen & (place <= spot)
                piece = jnp.where(seen, 0.0, HIDDEN)
                if kind == "own" and j > i:
                    piece = jnp.full((TILE, TILE), HIDDEN, F32)
                bias[at // TILE + j, part, :] = piece
        at += rows
        masked = at // TILE

    def emit(head, top, mixed):
        upper, lower = mixed[:, 0:TILE], mixed[:, TILE:]
        if started:
            fade = jnp.exp2((stat[head] - top) * factor)
            upper = acc[head, :, 0:TILE] * fade + upper
            lower = acc[head, :, TILE:] * fade + lower
        if final:
            outs[0][head] = (upper / lower).astype(BF16)
        else:
            outs[0][head, :, 0:TILE] = upper
            outs[0][head, :, TILE:] = lower

    if not started:
        moves[2].wait()
    keep = None if final else outs[1]
    attend(q, keys, vals, masked, bias, factor, stat, keep, emit, *room)


def absorb(parts, final, queries, ids, state, kv_local, factor):
    qheads, rows, width = queries.shape
    total = 0
    masked = 0
    for kind, arrays in parts:
        total += sum(a.shape[0] for a in arrays) // (2 * kv_local) if kind == "prefix" else rows
        masked = masked if kind == "prefix" else total
    plan = {
        "old": bool(state),
        "final": final,
        "parts": [(kind, len(arrays)) for kind, arrays in parts],
    }
    operands = [queries, ids, *state]
    for kind, arrays in parts:
        operands.extend(arrays)
    if final:
        shape = (jax.ShapeDtypeStruct((qheads, rows, width), BF16),)
    else:
        shape = (
            jax.ShapeDtypeStruct((qheads, rows, 2 * TILE), F32),
            jax.ShapeDtypeStruct((qheads, rows, TILE), F32),
        )
    specs = [VM] * len(operands)
    extra = []
    if not state:
        for at in (0, 2, 3):
            operands[at] = pltpu.with_memory_space_constraint(operands[at], pltpu.HBM)
        specs = [HB, VM, HB, HB] + [VM] * (len(operands) - 4)
        shape += (jax.ShapeDtypeStruct(queries.shape, BF16),)
        block = pltpu.VMEM(parts[0][1][0].shape, BF16)
        extra = [block, block, pltpu.SemaphoreType.DMA((3,))]
    return pl.pallas_call(
        functools.partial(absorb_kernel, plan, kv_local, rows, factor),
        out_shape=shape,
        in_specs=specs,
        out_specs=(VM,) * len(shape),
        scratch_shapes=[
            pltpu.VMEM((kv_local, total // TILE, width, TILE), BF16),
            pltpu.VMEM((kv_local, total, width), BF16),
            pltpu.VMEM((rows * kv_local, width), F32),
            pltpu.VMEM((max(masked, TILE) // TILE, rows, TILE), F32),
            *working_room(rows, total),
            *extra,
        ],
        cost_estimate=pl.CostEstimate(
            flops=4 * rows * qheads * total * width,
            bytes_accessed=4 * 2**20,
            transcendentals=rows * qheads * total,
        ),
        compiler_params=pltpu.CompilerParams(vmem_limit_bytes=GRANT),
    )(*operands)


def working_room(rows, total):
    return [
        pltpu.VMEM((2, total // TILE, rows, TILE), F32),
        pltpu.VMEM((2, rows, TILE), F32),
        pltpu.VMEM((2, rows, TILE), F32),
        pltpu.VMEM((2, total // TILE, rows, TILE), BF16),
    ]


def shards(query_suffix, key_suffix, value_suffix, key_prefix, value_prefix, file_ids):
    rows, _, width = query_suffix.shape
    kv_local = key_suffix.shape[1]
    factor = math.log2(math.e) / math.sqrt(width)
    count = lax.axis_size("ctx")
    queries = query_suffix.transpose(1, 0, 2)
    k0 = key_suffix.reshape(rows * kv_local, width)
    v0 = value_suffix.reshape(rows * kv_local, width)
    ids = (file_ids + 1).astype(BF16).reshape(rows // TILE, TILE)
    ids = jnp.pad(ids, ((0, IDROWS - rows // TILE), (0, 0)))
    k1 = passed_on(k0, 1)
    v1 = passed_on(jnp.concatenate([v0, ids]), 1)
    kp = key_prefix.reshape(-1, width)
    vp = value_prefix.reshape(-1, width)
    kp_other = swapped(kp, "pair", 1)
    vp_other = swapped(vp, "pair", 1)
    positions = key_prefix.shape[0]
    mine = pl.pallas_call(
        functools.partial(choose_kernel, kv_local),
        out_shape=jax.ShapeDtypeStruct((4 * kv_local * positions, width), BF16),
        in_specs=[HB, HB, VM, VM],
        out_specs=VM,
        scratch_shapes=[
            pltpu.VMEM((2,) + kp.shape, F32),
            pltpu.VMEM(kp.shape, BF16),
            pltpu.VMEM(vp.shape, BF16),
            pltpu.SemaphoreType.DMA((2,)),
        ],
        cost_estimate=pl.CostEstimate(flops=0, bytes_accessed=4 * kp.size * 2, transcendentals=0),
        compiler_params=pltpu.CompilerParams(vmem_limit_bytes=GRANT),
        name="choose",
    )(
        pltpu.with_memory_space_constraint(kp, pltpu.HBM),
        pltpu.with_memory_space_constraint(vp, pltpu.HBM),
        kp_other,
        vp_other,
    )
    k2 = passed_on(k1, 2)
    v2 = passed_on(v1, 2)
    prefix = [mine]
    bit = 1
    while bit < count:
        whole = jnp.concatenate(prefix) if len(prefix) > 1 else mine
        prefix.append(swapped(whole, "ctx", bit))
        bit *= 2
    rest = (kv_local, factor)
    early = [("own", [k0, v0]), ("back1", [k1, v1])]
    *state, queries = absorb(early, False, queries, ids, (), *rest)
    args = (queries, ids)
    late = [("back2", [k2, v2]), ("prefix", prefix[:-1])]
    state = absorb(late, False, *args, state, *rest)
    (out,) = absorb([("prefix", prefix[-1:])], True, *args, state, *rest)
    return out.transpose(1, 0, 2)


def solution(mesh):
    in_specs = (
        P(("groups", "ctx"), ("head", "pair"), None),
        P(("groups", "ctx"), ("head", "pair"), None),
        P(("groups", "ctx"), ("head", "pair"), None),
        P(("groups", "ctx", "pair"), "head", None),
        P(("groups", "ctx", "pair"), "head", None),
        P(("groups", "ctx")),
    )
    out_specs = P(("groups", "ctx"), ("head", "pair"), None)

    return jax.shard_map(shards, mesh=mesh, in_specs=in_specs, out_specs=out_specs, check_vma=False)
```

profile of v0, /device:TPU:16, one launch (start us, length us, event | category | flops | bytes accessed | tf_op | source)
XLA Modules:
  0.0 39.7 jit_solution(7397413838408585359)
XLA Ops:
  0.0 0.7 %fusion = bf16[3,128]{1,0:T(4,128)(2,1)S(1)} fusion(s32[384]{0:T(512)} %param.11), kind=kLoop, calls=%fused_computation.3 | loop fusion | flops 768 | bytes 2304 | tf_op jit(solution)/shard_map/reshape | solution.py:304
  0.7 0.9 %pad_maximum_fusion.1 = bf16[784,128]{1,0:T(8,128)(2,1)S(1)} fusion(bf16[16,128]{1,0:T(8,128)(2,1)S(1)} %pad.4.refs_1_, bf16[768,128]{1,0:T(8,128)(2,1)} %bitcast.8), kind=kLoop, calls=%fused_computation.1 | loop fusion | flops 401408 | bytes 401408 | tf_op jit(solution)/shard_map/concatenate | solution.py:307
  1.6 1.6 %collective-permute-start.1 = (bf16[784,128]{1,0:T(8,128)(2,1)S(1)}, bf16[784,128]{1,0:T(8,128)(2,1)S(1)}, u32[]{:S(2)}, u32[]{:S(2)}) collective-permute-start(bf16[784,128]{1,0:T(8,128)(2,1)S(1)} %pad_maximum_fusion.1), channel_id=1, source_target_pairs={{0,4},{4,8},{8,12},{12,0},{1,5},{5,9},{9,13},{13,1},{2,6},{6,10},{... | collective-permute-start | bytes 602120 | tf_op jit(solution)/shard_map/ppermute | solution.py:29
  3.3 0.1 collective-permute-start
  3.3 0.0 collective-permute-start.4
  3.3 0.5 %collective-permute-start.5 = (bf16[256,128]{1,0:T(8,128)(2,1)}, bf16[256,128]{1,0:T(8,128)(2,1)S(1)}, u32[]{:S(2)}, u32[]{:S(2)}) collective-permute-start(bf16[256,128]{1,0:T(8,128)(2,1)} %bitcast.12), channel_id=1, source_target_pairs={{0,1},{1,0},{2,3},{3,2},{4,5},{5,4},{6,7},{7,6},{8,9},{9,8},{10,11... | collective-permute-start | bytes 196616 | tf_op jit(solution)/shard_map/ppermute | solution.py:34
  3.8 1.0 %collective-permute-done.4.other_k = bf16[256,128]{1,0:T(8,128)(2,1)S(1)} collective-permute-done((bf16[256,128]{1,0:T(8,128)(2,1)}, bf16[256,128]{1,0:T(8,128)(2,1)S(1)}, u32[]{:S(2)}, u32[]{:S(2)}) %collective-permute-start.4) | collective-permute-done | bytes 65568 | tf_op jit(solution)/shard_map/ppermute | solution.py:34
  4.8 0.2 collective-permute-done.5.other_v
  5.0 1.0 %choose.1.refs_6_ = bf16[512,128]{1,0:T(8,128)(2,1)S(1)} custom-call(bf16[256,128]{1,0:T(8,128)(2,1)} %bitcast.11, bf16[256,128]{1,0:T(8,128)(2,1)} %bitcast.13, bf16[256,128]{1,0:T(8,128)(2,1)S(1)} %collective-permute-done.4.other_k, bf16[256,128]{1,0:T(8,128)(2,1)S(1)} %collective-permute-done.5.other_v), custom_call_target="tpu_custom_call" | custom-call | bytes 262144 | tf_op jit(solution)/shard_map/choose/pallas_call | solution.py:313
  5.9 1.8 %collective-permute-start.6 = (bf16[512,128]{1,0:T(8,128)(2,1)S(1)}, bf16[512,128]{1,0:T(8,128)(2,1)S(1)}, u32[]{:S(2)}, u32[]{:S(2)}) collective-permute-start(bf16[512,128]{1,0:T(8,128)(2,1)S(1)} %choose.1.refs_6_), channel_id=1, source_target_pairs={{0,4},{4,0},{8,12},{12,8},{1,5},{5,1},{9,13},{13,9},{2,6},{6,2},{1... | collective-permute-start | bytes 393224 | tf_op jit(solution)/shard_map/ppermute | solution.py:34
  7.7 5.2 %collective-permute-done.refs_4_ = bf16[768,128]{1,0:T(8,128)(2,1)S(1)} collective-permute-done((bf16[768,128]{1,0:T(8,128)(2,1)}, bf16[768,128]{1,0:T(8,128)(2,1)S(1)}, u32[]{:S(2)}, u32[]{:S(2)}) %collective-permute-start) | collective-permute-done | bytes 196640 | tf_op jit(solution)/shard_map/ppermute | solution.py:29
  13.0 4.3 %collective-permute-start.2 = (bf16[768,128]{1,0:T(8,128)(2,1)S(1)}, bf16[768,128]{1,0:T(8,128)(2,1)S(1)}, u32[]{:S(2)}, u32[]{:S(2)}) collective-permute-start(bf16[768,128]{1,0:T(8,128)(2,1)S(1)} %collective-permute-done.refs_4_), channel_id=1, source_target_pairs={{4,8},{8,12},{5,9},{9,13},{6,10},{10,14},{7,11},{11,15},{20,24},{2... | collective-permute-start | bytes 589832 | tf_op jit(solution)/shard_map/ppermute | solution.py:29
  17.2 0.0 collective-permute-done.1.refs_5_
  17.3 1.9 %collective-permute-start.3 = (bf16[784,128]{1,0:T(8,128)(2,1)S(1)}, bf16[784,128]{1,0:T(8,128)(2,1)S(1)}, u32[]{:S(2)}, u32[]{:S(2)}) collective-permute-start(bf16[784,128]{1,0:T(8,128)(2,1)S(1)} %collective-permute-done.1.refs_5_), channel_id=1, source_target_pairs={{4,8},{8,12},{5,9},{9,13},{6,10},{10,14},{7,11},{11,15},{20,24},{2... | collective-permute-start | bytes 602120 | tf_op jit(solution)/shard_map/ppermute | solution.py:29
  19.2 0.0 collective-permute-done.6.refs_7_
  19.2 0.1 collective-permute-start.7
  19.3 6.4 %shard_map.64 = (f32[10,384,256]{2,1,0:T(8,128)S(1)}, f32[10,384,128]{2,1,0:T(8,128)S(1)}, bf16[10,384,128]{2,1,0:T(8,128)(2,1)S(1)}) custom-call(bf16[10,384,128]{2,1,0:T(8,128)(2,1)} %bitcast.14, bf16[16,128]{1,0:T(8,128)(2,1)S(1)} %pad.4.refs_1_, bf16[768,128]{1,0:T(8,128)(2,1)} %bitcast.16, bf16[768,128]{1,0:T(8,128)(2,1)} %bitcast.9, ...), custom_call_target="tpu_custom_call" | custom-call | flops 1509949440 | bytes 4194304 | tf_op jit(solution)/shard_map/pallas_call | solution.py:265
  25.8 1.6 %collective-permute-done.2.refs_4_ = bf16[768,128]{1,0:T(8,128)(2,1)S(1)} collective-permute-done((bf16[768,128]{1,0:T(8,128)(2,1)S(1)}, bf16[768,128]{1,0:T(8,128)(2,1)S(1)}, u32[]{:S(2)}, u32[]{:S(2)}) %collective-permute-start.2) | collective-permute-done | bytes 196640 | tf_op jit(solution)/shard_map/ppermute | solution.py:29
  27.3 4.3 %collective-permute-done.3.refs_5_ = bf16[784,128]{1,0:T(8,128)(2,1)S(1)} collective-permute-done((bf16[784,128]{1,0:T(8,128)(2,1)S(1)}, bf16[784,128]{1,0:T(8,128)(2,1)S(1)}, u32[]{:S(2)}, u32[]{:S(2)}) %collective-permute-start.3) | collective-permute-done | bytes 200736 | tf_op jit(solution)/shard_map/ppermute | solution.py:29
  31.6 4.7 %shard_map.65 = (f32[10,384,256]{2,1,0:T(8,128)S(1)}, f32[10,384,128]{2,1,0:T(8,128)S(1)}) custom-call(bf16[10,384,128]{2,1,0:T(8,128)(2,1)S(1)} %get-tuple-element.10.refs_0_, bf16[16,128]{1,0:T(8,128)(2,1)S(1)} %pad.4.refs_1_, f32[10,384,256]{2,1,0:T(8,128)S(1)} %get-tuple-element.11.refs_2_, f32[10,384,128]{2,1,0:T(8,128)S(1)} %get-tuple-element.12.refs_3_, ...), custom_call_target="tpu_custom_call" | custom-call | flops 1258291200 | bytes 4194304 | tf_op jit(solution)/shard_map/pallas_call | solution.py:265
  36.3 0.0 collective-permute-done.7.refs_4_
  36.3 3.4 %shard_map.66 = bf16[10,384,128]{2,1,0:T(8,128)(2,1)} custom-call(bf16[10,384,128]{2,1,0:T(8,128)(2,1)S(1)} %get-tuple-element.10.refs_0_, bf16[16,128]{1,0:T(8,128)(2,1)S(1)} %pad.4.refs_1_, f32[10,384,256]{2,1,0:T(8,128)S(1)} %get-tuple-element.13.refs_2_, f32[10,384,128]{2,1,0:T(8,128)S(1)} %get-tuple-element.14.refs_3_, ...), custom_call_target="tpu_custom_call" | custom-call | flops 503316480 | bytes 4194304 | tf_op jit(solution)/shard_map/pallas_call | solution.py:265
  (2 shorter events, 0.0 us)
Async XLA Ops:
  1.6 15.6 %collective-permute-start.1 = (bf16[784,128]{1,0:T(8,128)(2,1)S(1)}, bf16[784,128]{1,0:T(8,128)(2,1)S(1)}, u32[]{:S(2)}, u32[]{:S(2)}) collective-permute-start(bf16[784,128]{1,0:T(8,128)(2,1)S(1)} %pad_maximum_fusion.1), channel_id=1, source_target_pairs={{0,4},{4,8},{8,12},{12,0},{1,5},{5,9},{9,13},{13,1},{2,6},{6,10},{... | collective-permute-start | bytes 602120 | tf_op jit(solution)/shard_map/ppermute | solution.py:29
  3.3 9.7 %collective-permute-start = (bf16[768,128]{1,0:T(8,128)(2,1)}, bf16[768,128]{1,0:T(8,128)(2,1)S(1)}, u32[]{:S(2)}, u32[]{:S(2)}) collective-permute-start(bf16[768,128]{1,0:T(8,128)(2,1)} %bitcast.15), channel_id=1, source_target_pairs={{0,4},{4,8},{8,12},{12,0},{1,5},{5,9},{9,13},{13,1},{2,6},{6,10},{... | collective-permute-start | bytes 589832 | tf_op jit(solution)/shard_map/ppermute | solution.py:29
  3.3 1.5 %collective-permute-start.4 = (bf16[256,128]{1,0:T(8,128)(2,1)}, bf16[256,128]{1,0:T(8,128)(2,1)S(1)}, u32[]{:S(2)}, u32[]{:S(2)}) collective-permute-start(bf16[256,128]{1,0:T(8,128)(2,1)} %bitcast.10), channel_id=1, source_target_pairs={{0,1},{1,0},{2,3},{3,2},{4,5},{5,4},{6,7},{7,6},{8,9},{9,8},{10,11... | collective-permute-start | bytes 196616 | tf_op jit(solution)/shard_map/ppermute | solution.py:34
  3.3 1.6 %collective-permute-start.5 = (bf16[256,128]{1,0:T(8,128)(2,1)}, bf16[256,128]{1,0:T(8,128)(2,1)S(1)}, u32[]{:S(2)}, u32[]{:S(2)}) collective-permute-start(bf16[256,128]{1,0:T(8,128)(2,1)} %bitcast.12), channel_id=1, source_target_pairs={{0,1},{1,0},{2,3},{3,2},{4,5},{5,4},{6,7},{7,6},{8,9},{9,8},{10,11... | collective-permute-start | bytes 196616 | tf_op jit(solution)/shard_map/ppermute | solution.py:34
  5.9 13.3 %collective-permute-start.6 = (bf16[512,128]{1,0:T(8,128)(2,1)S(1)}, bf16[512,128]{1,0:T(8,128)(2,1)S(1)}, u32[]{:S(2)}, u32[]{:S(2)}) collective-permute-start(bf16[512,128]{1,0:T(8,128)(2,1)S(1)} %choose.1.refs_6_), channel_id=1, source_target_pairs={{0,4},{4,0},{8,12},{12,8},{1,5},{5,1},{9,13},{13,9},{2,6},{6,2},{1... | collective-permute-start | bytes 393224 | tf_op jit(solution)/shard_map/ppermute | solution.py:34
  13.0 14.4 %collective-permute-start.2 = (bf16[768,128]{1,0:T(8,128)(2,1)S(1)}, bf16[768,128]{1,0:T(8,128)(2,1)S(1)}, u32[]{:S(2)}, u32[]{:S(2)}) collective-permute-start(bf16[768,128]{1,0:T(8,128)(2,1)S(1)} %collective-permute-done.refs_4_), channel_id=1, source_target_pairs={{4,8},{8,12},{5,9},{9,13},{6,10},{10,14},{7,11},{11,15},{20,24},{2... | collective-permute-start | bytes 589832 | tf_op jit(solution)/shard_map/ppermute | solution.py:29
  17.3 14.4 %collective-permute-start.3 = (bf16[784,128]{1,0:T(8,128)(2,1)S(1)}, bf16[784,128]{1,0:T(8,128)(2,1)S(1)}, u32[]{:S(2)}, u32[]{:S(2)}) collective-permute-start(bf16[784,128]{1,0:T(8,128)(2,1)S(1)} %collective-permute-done.1.refs_5_), channel_id=1, source_target_pairs={{4,8},{8,12},{5,9},{9,13},{6,10},{10,14},{7,11},{11,15},{20,24},{2... | collective-permute-start | bytes 602120 | tf_op jit(solution)/shard_map/ppermute | solution.py:29
  19.2 17.1 %collective-permute-start.7 = (bf16[1024,128]{1,0:T(8,128)(2,1)S(1)}, bf16[1024,128]{1,0:T(8,128)(2,1)S(1)}, u32[]{:S(2)}, u32[]{:S(2)}) collective-permute-start(bf16[1024,128]{1,0:T(8,128)(2,1)S(1)} %pad_maximum_fusion), channel_id=1, source_target_pairs={{0,8},{4,12},{8,0},{12,4},{1,9},{5,13},{9,1},{13,5},{2,10},{6,14},... | collective-permute-start | bytes 786440 | tf_op jit(solution)/shard_map/ppermute | solution.py:34
where the time goes:
time: 40 us; the launch traced here: 39.7 us
  Pallas kernels  15.4 us (38%)
  waiting for transfers between devices  12.2 us (30%)
  starting transfers between devices  10.3 us (26%)
  other arithmetic  1.64 us (4%)
    pallas_call x3, Pallas kernels, absorb(): pl.pallas_call(functools.partial(absorb_kernel, plan, kv_local, rows, fac...  14.5 us
    ppermute x4, waiting for transfers between devices, passed_on(): return lax.ppermute(value, 'ctx', pairs)  11.1 us
    ppermute x4, starting transfers between devices, passed_on(): return lax.ppermute(value, 'ctx', pairs)  7.89 us
    ppermute x4, starting transfers between devices, swapped(): return lax.ppermute(value, axis, [(i, i ^ bit) for i in range(count)])  2.38 us
    ppermute x4, waiting for transfers between devices, swapped(): return lax.ppermute(value, axis, [(i, i ^ bit) for i in range(count)])  1.12 us
    pallas_call x1, Pallas kernels, shards(): pl.pallas_call(functools.partial(choose_kernel, kv_local), out_shape=jax....  0.95 us
    concatenate x1, other arithmetic, shards(): v1 = passed_on(jnp.concatenate([v0, ids]), 1)  0.94 us
  transfers between devices with their start and end apart: 8, of which 5 were waited for; matrix products, arithmetic and copies ran while one was open for 0% of the time, Pallas kernels for 30%

commit v1 on v0

--- a/solution.py
+++ b/solution.py
@@ -13,6 +13,7 @@
 TILE = 128
 IDROWS = 16
 CHUNK = 32
+UNROLL = 4
 GRANT = 24 * 2**20
 F32 = jnp.float32
 BF16 = jnp.bfloat16
@@ -44,7 +45,7 @@
     for head in range(heads):
         picked = one_head_rows(src, 0, rows, heads, wide, head)
         for j in range(0, rows, TILE):
-            keys[head, (at + j) // TILE] = jnp.transpose(picked[j : j + TILE, :]).astype(BF16)
+            keys[head, (at + j) // TILE] = jnp.transpose(picked[j : j + TILE, :].astype(BF16))
 
 
 def place_values(src, rows, heads, wide, vals, at):
@@ -131,16 +132,15 @@
     score(0, 0)
     score(1, 1)
     weigh(0, 0)
-    trips = (qheads - 2) // 2
+    trips = (qheads - 2) // UNROLL
 
     def trip(index, _):
-        head = 1 + 2 * index
-        step(head, 1)
-        step(head + 1, 0)
+        for ahead in range(1, UNROLL + 1):
+            step(UNROLL * index + ahead, ahead % 2)
         return 0
 
     lax.fori_loop(0, trips, trip, 0)
-    for head in range(1 + 2 * trips, qheads - 1):
+    for head in range(1 + UNROLL * trips, qheads - 1):
         step(head, head % 2)
     last = qheads - 1
     weigh(last, last % 2)
@@ -169,66 +169,97 @@
         ]
         for move in moves:
             move.start()
-        moves[0].wait()
-        moves[1].wait()
         q = landed
+    if plan["skips"]:
+        acc, stat = outs
+    if final:
+        ready, leaving = refs[-2:]
+        refs = refs[:-2]
     keys, vals, wide, bias, *room = refs
-    tiles = rows // TILE
-    mine = ids[...]
-    at = 0
-    masked = 0
-    for kind, taken in sources:
-        if kind == "prefix":
-            size = 2 * kv_local * TILE
-            for chunk in taken:
-                for first in range(0, chunk.shape[0], size):
-                    for head in range(kv_local):
-                        low = first + head * TILE
-                        keys[head, at // TILE] = jnp.transpose(chunk[low : low + TILE, :])
-                        low = first + (kv_local + head) * TILE
-                        vals[head, at : at + TILE, :] = chunk[low : low + TILE, :]
-                    at += TILE
-            continue
-        place_keys(taken[0], rows, kv_local, wide, keys, at)
-        place_values(taken[1], rows, kv_local, wide, vals, at)
-        if kind == "own":
-            other = mine
-            spot = lax.broadcasted_iota(jnp.int32, (TILE, TILE), 0)
-            place = lax.broadcasted_iota(jnp.int32, (TILE, TILE), 1)
-        else:
-            hops = 1 if kind == "back1" else 2
-            other = taken[1][rows * kv_local : rows * kv_local + IDROWS, :].astype(F32)
-            other = jnp.where(lax.axis_index("ctx") >= hops, other, 0.0)
-        for i in range(tiles):
-            column = id_column(mine, i)
-            part = slice(i * TILE, (i + 1) * TILE)
-            for j in range(tiles):
-                seen = column == id_row(other, j)
-                if kind == "own" and j == i:
-                    seen = seen & (place <= spot)
-                piece = jnp.where(seen, 0.0, HIDDEN)
-                if kind == "own" and j > i:
-                    piece = jnp.full((TILE, TILE), HIDDEN, F32)
-                bias[at // TILE + j, part, :] = piece
-        at += rows
-        masked = at // TILE
-
-    def emit(head, top, mixed):
-        upper, lower = mixed[:, 0:TILE], mixed[:, TILE:]
-        if started:
-            fade = jnp.exp2((stat[head] - top) * factor)
-            upper = acc[head, :, 0:TILE] * fade + upper
-            lower = acc[head, :, TILE:] * fade + lower
-        if final:
-            outs[0][head] = (upper / lower).astype(BF16)
-        else:
-            outs[0][head, :, 0:TILE] = upper
-            outs[0][head, :, TILE:] = lower
-
-    if not started:
-        moves[2].wait()
-    keep = None if final else outs[1]
-    attend(q, keys, vals, masked, bias, factor, stat, keep, emit, *room)
+
+    def visible_at_all():
+        source = sources[0][1][1]
+        last = source[rows * kv_local : rows * kv_local + IDROWS, :].astype(F32)
+        apart = last[rows // TILE - 1 : rows // TILE, TILE - 1 :] - ids[...].astype(F32)[0:1, 0:1]
+        return (lax.axis_index("ctx") >= 2) & (jnp.max(jnp.abs(apart)) < 0.5)
+
+    def work():
+        tiles = rows // TILE
+        mine = ids[...]
+        at = 0
+        masked = 0
+        places = []
+        for kind, taken in sources:
+            places.append((kind == "own", at, kind, taken))
+            if kind == "prefix":
+                at += sum(chunk.shape[0] for chunk in taken) // (2 * kv_local)
+            else:
+                at += rows
+                masked = at // TILE
+        for own, at, kind, taken in sorted(places, key=lambda place: place[:2]):
+            if kind == "prefix":
+                size = 2 * kv_local * TILE
+                for chunk in taken:
+                    for first in range(0, chunk.shape[0], size):
+                        for head in range(kv_local):
+                            low = first + head * TILE
+                            keys[head, at // TILE] = jnp.transpose(chunk[low : low + TILE, :])
+                            low = first + (kv_local + head) * TILE
+                            vals[head, at : at + TILE, :] = chunk[low : low + TILE, :]
+                        at += TILE
+                continue
+            if kind == "own":
+                other = mine
+                spot = lax.broadcasted_iota(jnp.int32, (TILE, TILE), 0)
+                place = lax.broadcasted_iota(jnp.int32, (TILE, TILE), 1)
+            else:
+                hops = 1 if kind == "back1" else 2
+                other = taken[1][rows * kv_local : rows * kv_local + IDROWS, :].astype(F32)
+                other = jnp.where(lax.axis_index("ctx") >= hops, other, 0.0)
+            for i in range(tiles):
+                column = id_column(mine, i)
+                part = slice(i * TILE, (i + 1) * TILE)
+                for j in range(tiles):
+                    seen = column == id_row(other, j)
+                    if kind == "own" and j == i:
+                        seen = seen & (place <= spot)
+                    piece = jnp.where(seen, 0.0, HIDDEN)
+                    if kind == "own" and j > i:
+                        piece = jnp.full((TILE, TILE), HIDDEN, F32)
+                    bias[at // TILE + j, part, :] = piece
+            if own:
+                moves[0].wait()
+                moves[1].wait()
+            place_keys(taken[0], rows, kv_local, wide, keys, at)
+            place_values(taken[1], rows, kv_local, wide, vals, at)
+
+        def emit(head, top, mixed):
+            upper, lower = mixed[:, 0:TILE], mixed[:, TILE:]
+            if started:
+                fade = jnp.exp2((stat[head] - top) * factor)
+                upper = acc[head, :, 0:TILE] * fade + upper
+                lower = acc[head, :, TILE:] * fade + lower
+            if final:
+                ready[head] = (upper / lower).astype(BF16)
+                pltpu.make_async_copy(ready.at[head], outs[0].at[head], leaving.at[head]).start()
+            else:
+                outs[0][head, :, 0:TILE] = upper
+                outs[0][head, :, TILE:] = lower
+                if started:
+                    outs[1][head] = top
+
+        if not started:
+            moves[2].wait()
+        keep = None if final or plan["skips"] else outs[1]
+        attend(q, keys, vals, masked, bias, factor, stat, keep, emit, *room)
+
+    if plan["skips"]:
+        pl.when(visible_at_all())(work)
+    else:
+        work()
+    if final:
+        for head in range(q.shape[0]):
+            pltpu.make_async_copy(ready.at[head], outs[0].at[head], leaving.at[head]).wait()
 
 
 def absorb(parts, final, queries, ids, state, kv_local, factor):
@@ -241,6 +272,7 @@
     plan = {
         "old": bool(state),
         "final": final,
+        "skips": [kind for kind, _ in parts] == ["back2"] and not final,
         "parts": [(kind, len(arrays)) for kind, arrays in parts],
     }
     operands = [queries, ids, *state]
@@ -262,11 +294,19 @@
         shape += (jax.ShapeDtypeStruct(queries.shape, BF16),)
         block = pltpu.VMEM(parts[0][1][0].shape, BF16)
         extra = [block, block, pltpu.SemaphoreType.DMA((3,))]
+    out_specs = (VM,) * len(shape)
+    aliases = {}
+    if final:
+        out_specs = (HB,)
+        extra = [pltpu.VMEM(shape[0].shape, BF16), pltpu.SemaphoreType.DMA((qheads,))]
+    elif plan["skips"]:
+        aliases = {2: 0, 3: 1}
     return pl.pallas_call(
         functools.partial(absorb_kernel, plan, kv_local, rows, factor),
         out_shape=shape,
         in_specs=specs,
-        out_specs=(VM,) * len(shape),
+        out_specs=out_specs,
+        input_output_aliases=aliases,
         scratch_shapes=[
             pltpu.VMEM((kv_local, total // TILE, width, TILE), BF16),
             pltpu.VMEM((kv_local, total, width), BF16),
@@ -333,17 +373,17 @@
     k2 = passed_on(k1, 2)
     v2 = passed_on(v1, 2)
     prefix = [mine]
-    bit = 1
-    while bit < count:
+    bit = count // 2
+    while bit:
         whole = jnp.concatenate(prefix) if len(prefix) > 1 else mine
         prefix.append(swapped(whole, "ctx", bit))
-        bit *= 2
+        bit //= 2
     rest = (kv_local, factor)
-    early = [("own", [k0, v0]), ("back1", [k1, v1])]
-    *state, queries = absorb(early, False, queries, ids, (), *rest)
+    *state, queries = absorb([("own", [k0, v0])], False, queries, ids, (), *rest)
     args = (queries, ids)
-    late = [("back2", [k2, v2]), ("prefix", prefix[:-1])]
-    state = absorb(late, False, *args, state, *rest)
+    near = [("back1", [k1, v1]), ("prefix", prefix[:-1])]
+    state = absorb(near, False, *args, state, *rest)
+    state = absorb([("back2", [k2, v2])], False, *args, state, *rest)
     (out,) = absorb([("prefix", prefix[-1:])], True, *args, state, *rest)
     return out.transpose(1, 0, 2)
 

time: 40 us -> 37.3 us (0.932)
  the two profiles are of different devices: /device:TPU:16 before, /device:TPU:0 now
where the time goes in v1:
time: 37.3 us; the launch traced here: 37.1 us
  Pallas kernels  12.8 us (34%)
  waiting for transfers between devices  11.5 us (31%)
  starting transfers between devices  11 us (29%)
  other arithmetic  1.64 us (4%)
    pallas_call x4, Pallas kernels, absorb(): pl.pallas_call(functools.partial(absorb_kernel, plan, kv_local, rows, fac...  11.9 us
    ppermute x4, waiting for transfers between devices, passed_on(): return lax.ppermute(value, 'ctx', pairs)  6.94 us
    ppermute x4, starting transfers between devices, passed_on(): return lax.ppermute(value, 'ctx', pairs)  6.02 us
    ppermute x4, starting transfers between devices, swapped(): return lax.ppermute(value, axis, [(i, i ^ bit) for i in range(count)])  5.01 us
    ppermute x4, waiting for transfers between devices, swapped(): return lax.ppermute(value, axis, [(i, i ^ bit) for i in range(count)])  4.55 us
    pallas_call x1, Pallas kernels, shards(): pl.pallas_call(functools.partial(choose_kernel, kv_local), out_shape=jax....  0.95 us
    concatenate x1, other arithmetic, shards(): v1 = passed_on(jnp.concatenate([v0, ids]), 1)  0.94 us
  transfers between devices with their start and end apart: 8, of which 3 were waited for; matrix products, arithmetic and copies ran while one was open for 0% of the time, Pallas kernels for 27%

profile of v1, /device:TPU:0, one launch (start us, length us, event | category | flops | bytes accessed | tf_op | source)
XLA Modules:
  0.0 37.1 jit_solution(13392813665070823350)
XLA Ops:
  0.0 0.7 %fusion = bf16[3,128]{1,0:T(4,128)(2,1)S(1)} fusion(s32[384]{0:T(512)} %param.11), kind=kLoop, calls=%fused_computation.3 | loop fusion | flops 768 | bytes 2304 | tf_op jit(solution)/shard_map/reshape | solution.py:344
  0.7 0.9 %pad_maximum_fusion.1 = bf16[784,128]{1,0:T(8,128)(2,1)S(1)} fusion(bf16[16,128]{1,0:T(8,128)(2,1)S(1)} %pad.4.refs_1_, bf16[768,128]{1,0:T(8,128)(2,1)} %bitcast.8), kind=kLoop, calls=%fused_computation.1 | loop fusion | flops 401408 | bytes 401408 | tf_op jit(solution)/shard_map/concatenate | solution.py:347
  1.6 3.1 %collective-permute-start.1 = (bf16[784,128]{1,0:T(8,128)(2,1)S(1)}, bf16[784,128]{1,0:T(8,128)(2,1)S(1)}, u32[]{:S(2)}, u32[]{:S(2)}) collective-permute-start(bf16[784,128]{1,0:T(8,128)(2,1)S(1)} %pad_maximum_fusion.1), channel_id=1, source_target_pairs={{0,4},{4,8},{8,12},{12,0},{1,5},{5,9},{9,13},{13,1},{2,6},{6,10},{... | collective-permute-start | bytes 602120 | tf_op jit(solution)/shard_map/ppermute | solution.py:30
  4.7 0.0 collective-permute-start.2
  4.7 1.6 %collective-permute-start = (bf16[768,128]{1,0:T(8,128)(2,1)}, bf16[768,128]{1,0:T(8,128)(2,1)S(1)}, u32[]{:S(2)}, u32[]{:S(2)}) collective-permute-start(bf16[768,128]{1,0:T(8,128)(2,1)} %bitcast.15), channel_id=1, source_target_pairs={{0,4},{4,8},{8,12},{12,0},{1,5},{5,9},{9,13},{13,1},{2,6},{6,10},{... | collective-permute-start | bytes 589832 | tf_op jit(solution)/shard_map/ppermute | solution.py:30
  6.3 0.2 collective-permute-start.3
  6.6 0.0 collective-permute-done.2.other_k
  6.6 1.2 %collective-permute-done.3.other_v = bf16[256,128]{1,0:T(8,128)(2,1)S(1)} collective-permute-done((bf16[256,128]{1,0:T(8,128)(2,1)}, bf16[256,128]{1,0:T(8,128)(2,1)S(1)}, u32[]{:S(2)}, u32[]{:S(2)}) %collective-permute-start.3) | collective-permute-done | bytes 65568 | tf_op jit(solution)/shard_map/ppermute | solution.py:35
  7.8 1.0 %choose.1.refs_6_ = bf16[512,128]{1,0:T(8,128)(2,1)S(1)} custom-call(bf16[256,128]{1,0:T(8,128)(2,1)} %bitcast.11, bf16[256,128]{1,0:T(8,128)(2,1)} %bitcast.13, bf16[256,128]{1,0:T(8,128)(2,1)S(1)} %collective-permute-done.2.other_k, bf16[256,128]{1,0:T(8,128)(2,1)S(1)} %collective-permute-done.3.other_v), custom_call_target="tpu_custom_call" | custom-call | bytes 262144 | tf_op jit(solution)/shard_map/choose/pallas_call | solution.py:353
  8.8 1.2 %collective-permute-start.4 = (bf16[512,128]{1,0:T(8,128)(2,1)S(1)}, bf16[512,128]{1,0:T(8,128)(2,1)S(1)}, u32[]{:S(2)}, u32[]{:S(2)}) collective-permute-start(bf16[512,128]{1,0:T(8,128)(2,1)S(1)} %choose.1.refs_6_), channel_id=1, source_target_pairs={{0,8},{4,12},{8,0},{12,4},{1,9},{5,13},{9,1},{13,5},{2,10},{6,14},... | collective-permute-start | bytes 393224 | tf_op jit(solution)/shard_map/ppermute | solution.py:35
  10.0 6.9 %collective-permute-done.refs_4_ = bf16[768,128]{1,0:T(8,128)(2,1)S(1)} collective-permute-done((bf16[768,128]{1,0:T(8,128)(2,1)}, bf16[768,128]{1,0:T(8,128)(2,1)S(1)}, u32[]{:S(2)}, u32[]{:S(2)}) %collective-permute-start) | collective-permute-done | bytes 196640 | tf_op jit(solution)/shard_map/ppermute | solution.py:30
  16.9 0.7 %collective-permute-start.5 = (bf16[768,128]{1,0:T(8,128)(2,1)S(1)}, bf16[768,128]{1,0:T(8,128)(2,1)S(1)}, u32[]{:S(2)}, u32[]{:S(2)}) collective-permute-start(bf16[768,128]{1,0:T(8,128)(2,1)S(1)} %collective-permute-done.refs_4_), channel_id=1, source_target_pairs={{4,8},{8,12},{5,9},{9,13},{6,10},{10,14},{7,11},{11,15},{20,24},{2... | collective-permute-start | bytes 589832 | tf_op jit(solution)/shard_map/ppermute | solution.py:30
  17.6 0.0 collective-permute-done.1.refs_5_
  17.6 0.7 %collective-permute-start.6 = (bf16[784,128]{1,0:T(8,128)(2,1)S(1)}, bf16[784,128]{1,0:T(8,128)(2,1)S(1)}, u32[]{:S(2)}, u32[]{:S(2)}) collective-permute-start(bf16[784,128]{1,0:T(8,128)(2,1)S(1)} %collective-permute-done.1.refs_5_), channel_id=1, source_target_pairs={{4,8},{8,12},{5,9},{9,13},{6,10},{10,14},{7,11},{11,15},{20,24},{2... | collective-permute-start | bytes 602120 | tf_op jit(solution)/shard_map/ppermute | solution.py:30
  18.3 3.3 %collective-permute-done.4.refs_7_ = bf16[512,128]{1,0:T(8,128)(2,1)S(1)} collective-permute-done((bf16[512,128]{1,0:T(8,128)(2,1)S(1)}, bf16[512,128]{1,0:T(8,128)(2,1)S(1)}, u32[]{:S(2)}, u32[]{:S(2)}) %collective-permute-start.4) | collective-permute-done | bytes 131104 | tf_op jit(solution)/shard_map/ppermute | solution.py:35
  21.6 3.5 %collective-permute-start.7 = (bf16[1024,128]{1,0:T(8,128)(2,1)S(1)}, bf16[1024,128]{1,0:T(8,128)(2,1)S(1)}, u32[]{:S(2)}, u32[]{:S(2)}) collective-permute-start(bf16[1024,128]{1,0:T(8,128)(2,1)S(1)} %pad_maximum_fusion), channel_id=1, source_target_pairs={{0,4},{4,0},{8,12},{12,8},{1,5},{5,1},{9,13},{13,9},{2,6},{6,2},{1... | collective-permute-start | bytes 786440 | tf_op jit(solution)/shard_map/ppermute | solution.py:35
  25.2 4.1 %shard_map.64 = (f32[10,384,256]{2,1,0:T(8,128)S(1)}, f32[10,384,128]{2,1,0:T(8,128)S(1)}, bf16[10,384,128]{2,1,0:T(8,128)(2,1)S(1)}) custom-call(bf16[10,384,128]{2,1,0:T(8,128)(2,1)} %bitcast.14, bf16[16,128]{1,0:T(8,128)(2,1)S(1)} %pad.4.refs_1_, bf16[768,128]{1,0:T(8,128)(2,1)} %bitcast.16, bf16[768,128]{1,0:T(8,128)(2,1)} %bitcast.9), custom_call_target="tpu_custom_call" | custom-call | flops 754974720 | bytes 4194304 | tf_op jit(solution)/shard_map/pallas_call | solution.py:304
  29.2 4.6 %shard_map.65 = (f32[10,384,256]{2,1,0:T(8,128)S(1)}, f32[10,384,128]{2,1,0:T(8,128)S(1)}) custom-call(bf16[10,384,128]{2,1,0:T(8,128)(2,1)S(1)} %get-tuple-element.12.refs_0_, bf16[16,128]{1,0:T(8,128)(2,1)S(1)} %pad.4.refs_1_, f32[10,384,256]{2,1,0:T(8,128)S(1)} %get-tuple-element.13.refs_2_, f32[10,384,128]{2,1,0:T(8,128)S(1)} %get-tuple-element.14.refs_3_, ...), custom_call_target="tpu_custom_call" | custom-call | flops 1258291200 | bytes 4194304 | tf_op jit(solution)/shard_map/pallas_call | solution.py:304
  33.9 0.0 collective-permute-done.5.refs_4_
  33.9 0.0 collective-permute-done.6.refs_5_
  33.9 0.2 shard_map.66
  34.1 0.0 collective-permute-done.7.refs_4_
  34.1 3.0 %shard_map.67 = bf16[10,384,128]{2,1,0:T(8,128)(2,1)} custom-call(bf16[10,384,128]{2,1,0:T(8,128)(2,1)S(1)} %get-tuple-element.12.refs_0_, bf16[16,128]{1,0:T(8,128)(2,1)S(1)} %pad.4.refs_1_, f32[10,384,256]{2,1,0:T(8,128)S(1)} %get-tuple-element.17.refs_2_, f32[10,384,128]{2,1,0:T(8,128)S(1)} %get-tuple-element.18.refs_3_, ...), custom_call_target="tpu_custom_call" | custom-call | flops 503316480 | bytes 4194304 | tf_op jit(solution)/shard_map/pallas_call | solution.py:304
  (2 shorter events, 0.0 us)
Async XLA Ops:
  1.6 16.0 %collective-permute-start.1 = (bf16[784,128]{1,0:T(8,128)(2,1)S(1)}, bf16[784,128]{1,0:T(8,128)(2,1)S(1)}, u32[]{:S(2)}, u32[]{:S(2)}) collective-permute-start(bf16[784,128]{1,0:T(8,128)(2,1)S(1)} %pad_maximum_fusion.1), channel_id=1, source_target_pairs={{0,4},{4,8},{8,12},{12,0},{1,5},{5,9},{9,13},{13,1},{2,6},{6,10},{... | collective-permute-start | bytes 602120 | tf_op jit(solution)/shard_map/ppermute | solution.py:30
  4.7 1.8 %collective-permute-start.2 = (bf16[256,128]{1,0:T(8,128)(2,1)}, bf16[256,128]{1,0:T(8,128)(2,1)S(1)}, u32[]{:S(2)}, u32[]{:S(2)}) collective-permute-start(bf16[256,128]{1,0:T(8,128)(2,1)} %bitcast.10), channel_id=1, source_target_pairs={{0,1},{1,0},{2,3},{3,2},{4,5},{5,4},{6,7},{7,6},{8,9},{9,8},{10,11... | collective-permute-start | bytes 196616 | tf_op jit(solution)/shard_map/ppermute | solution.py:35
  4.7 12.2 %collective-permute-start = (bf16[768,128]{1,0:T(8,128)(2,1)}, bf16[768,128]{1,0:T(8,128)(2,1)S(1)}, u32[]{:S(2)}, u32[]{:S(2)}) collective-permute-start(bf16[768,128]{1,0:T(8,128)(2,1)} %bitcast.15), channel_id=1, source_target_pairs={{0,4},{4,8},{8,12},{12,0},{1,5},{5,9},{9,13},{13,1},{2,6},{6,10},{... | collective-permute-start | bytes 589832 | tf_op jit(solution)/shard_map/ppermute | solution.py:30
  6.3 1.5 %collective-permute-start.3 = (bf16[256,128]{1,0:T(8,128)(2,1)}, bf16[256,128]{1,0:T(8,128)(2,1)S(1)}, u32[]{:S(2)}, u32[]{:S(2)}) collective-permute-start(bf16[256,128]{1,0:T(8,128)(2,1)} %bitcast.12), channel_id=1, source_target_pairs={{0,1},{1,0},{2,3},{3,2},{4,5},{5,4},{6,7},{7,6},{8,9},{9,8},{10,11... | collective-permute-start | bytes 196616 | tf_op jit(solution)/shard_map/ppermute | solution.py:35
  8.8 12.8 %collective-permute-start.4 = (bf16[512,128]{1,0:T(8,128)(2,1)S(1)}, bf16[512,128]{1,0:T(8,128)(2,1)S(1)}, u32[]{:S(2)}, u32[]{:S(2)}) collective-permute-start(bf16[512,128]{1,0:T(8,128)(2,1)S(1)} %choose.1.refs_6_), channel_id=1, source_target_pairs={{0,8},{4,12},{8,0},{12,4},{1,9},{5,13},{9,1},{13,5},{2,10},{6,14},... | collective-permute-start | bytes 393224 | tf_op jit(solution)/shard_map/ppermute | solution.py:35
  16.9 17.0 %collective-permute-start.5 = (bf16[768,128]{1,0:T(8,128)(2,1)S(1)}, bf16[768,128]{1,0:T(8,128)(2,1)S(1)}, u32[]{:S(2)}, u32[]{:S(2)}) collective-permute-start(bf16[768,128]{1,0:T(8,128)(2,1)S(1)} %collective-permute-done.refs_4_), channel_id=1, source_target_pairs={{4,8},{8,12},{5,9},{9,13},{6,10},{10,14},{7,11},{11,15},{20,24},{2... | collective-permute-start | bytes 589832 | tf_op jit(solution)/shard_map/ppermute | solution.py:30
  17.6 16.3 %collective-permute-start.6 = (bf16[784,128]{1,0:T(8,128)(2,1)S(1)}, bf16[784,128]{1,0:T(8,128)(2,1)S(1)}, u32[]{:S(2)}, u32[]{:S(2)}) collective-permute-start(bf16[784,128]{1,0:T(8,128)(2,1)S(1)} %collective-permute-done.1.refs_5_), channel_id=1, source_target_pairs={{4,8},{8,12},{5,9},{9,13},{6,10},{10,14},{7,11},{11,15},{20,24},{2... | collective-permute-start | bytes 602120 | tf_op jit(solution)/shard_map/ppermute | solution.py:30
  21.6 12.5 %collective-permute-start.7 = (bf16[1024,128]{1,0:T(8,128)(2,1)S(1)}, bf16[1024,128]{1,0:T(8,128)(2,1)S(1)}, u32[]{:S(2)}, u32[]{:S(2)}) collective-permute-start(bf16[1024,128]{1,0:T(8,128)(2,1)S(1)} %pad_maximum_fusion), channel_id=1, source_target_pairs={{0,4},{4,0},{8,12},{12,8},{1,5},{5,1},{9,13},{13,9},{2,6},{6,2},{1... | collective-permute-start | bytes 786440 | tf_op jit(solution)/shard_map/ppermute | solution.py:35

commit v2 on v1

--- a/solution.py
+++ b/solution.py
@@ -13,7 +13,6 @@
 TILE = 128
 IDROWS = 16
 CHUNK = 32
-UNROLL = 4
 GRANT = 24 * 2**20
 F32 = jnp.float32
 BF16 = jnp.bfloat16
@@ -78,13 +77,20 @@
         for slot, src in enumerate((mine, other)):
             wide[slot] = src[...].astype(F32)
         for head in range(kv_local):
-            for slot in range(2):
-                picked = wide[slot, pl.ds(start + head, positions, stride=heads), :]
-                out[place : place + positions, :] = picked.astype(BF16)
-                place += positions
-
-
-def attend(q, keys, vals, masked, bias, factor, old, keep, emit, scores, peaks, tops, weights):
+            halves = [
+                wide[slot, pl.ds(start + head, positions, stride=heads), :].astype(BF16)
+                for slot in range(2)
+            ]
+            tile = jnp.concatenate(halves, axis=0)
+            if mine is own_k:
+                tile = jnp.transpose(tile)
+            out[place : place + TILE, :] = tile
+            place += TILE
+
+
+def attend(
+    q, keys, vals, masked, bias, factor, old, keep, emit, unroll, scores, peaks, tops, weights
+):
     qheads, rows, _ = q.shape
     blocks = keys.shape[1]
     group = qheads // keys.shape[0]
@@ -132,15 +138,15 @@
     score(0, 0)
     score(1, 1)
     weigh(0, 0)
-    trips = (qheads - 2) // UNROLL
+    trips = (qheads - 2) // unroll
 
     def trip(index, _):
-        for ahead in range(1, UNROLL + 1):
-            step(UNROLL * index + ahead, ahead % 2)
+        for ahead in range(1, unroll + 1):
+            step(unroll * index + ahead, ahead % 2)
         return 0
 
     lax.fori_loop(0, trips, trip, 0)
-    for head in range(1 + UNROLL * trips, qheads - 1):
+    for head in range(1 + unroll * trips, qheads - 1):
         step(head, head % 2)
     last = qheads - 1
     weigh(last, last % 2)
@@ -203,7 +209,7 @@
                     for first in range(0, chunk.shape[0], size):
                         for head in range(kv_local):
                             low = first + head * TILE
-                            keys[head, at // TILE] = jnp.transpose(chunk[low : low + TILE, :])
+                            keys[head, at // TILE] = chunk[low : low + TILE, :]
                             low = first + (kv_local + head) * TILE
                             vals[head, at : at + TILE, :] = chunk[low : low + TILE, :]
                         at += TILE
@@ -251,7 +257,7 @@
         if not started:
             moves[2].wait()
         keep = None if final or plan["skips"] else outs[1]
-        attend(q, keys, vals, masked, bias, factor, stat, keep, emit, *room)
+        attend(q, keys, vals, masked, bias, factor, stat, keep, emit, 8 if final else 4, *room)
 
     if plan["skips"]:
         pl.when(visible_at_all())(work)
@@ -372,11 +378,15 @@
     )
     k2 = passed_on(k1, 2)
     v2 = passed_on(v1, 2)
-    prefix = [mine]
+    prefix, arrived = [mine], []
     bit = count // 2
     while bit:
-        whole = jnp.concatenate(prefix) if len(prefix) > 1 else mine
-        prefix.append(swapped(whole, "ctx", bit))
+        groups = [prefix[:1], prefix[1:]] if bit == 1 else [prefix]
+        for group in groups:
+            whole = jnp.concatenate(group) if len(group) > 1 else group[0]
+            arrived.append(swapped(whole, "ctx", bit))
+        prefix = prefix + arrived
+        arrived = []
         bit //= 2
     rest = (kv_local, factor)
     *state, queries = absorb([("own", [k0, v0])], False, queries, ids, (), *rest)

time: 37.3 us -> 37.1 us (level)
  waiting for transfers between devices: 11.5 us -> 6.26 us
  starting transfers between devices: 11 us -> 16.2 us
    ppermute x4 -> x5, starting transfers between devices: 5.01 us -> 10.2 us  [swapped(): return lax.ppermute(value, axis, [(i, i ^ bit) for i in range(count)])]
    ppermute x4 -> x5, waiting for transfers between devices: 4.55 us -> 1.12 us  [swapped(): return lax.ppermute(value, axis, [(i, i ^ bit) for i in range(count)])]
    ppermute x4, waiting for transfers between devices: 6.94 us -> 5.14 us  [passed_on(): return lax.ppermute(value, 'ctx', pairs)]
  transfers between devices with their start and end apart: 8 -> 9, of which waited for: 3 -> 3; matrix products, arithmetic and copies ran while one was open for 0% -> 0% of each run, Pallas kernels for 27% -> 28%
where the time goes in v2:
time: 37.1 us; the launch traced here: 36.8 us
  starting transfers between devices  16.2 us (44%)
  Pallas kernels  12.7 us (34%)
  waiting for transfers between devices  6.26 us (17%)
  other arithmetic  1.63 us (4%)
    pallas_call x4, Pallas kernels, absorb(): pl.pallas_call(functools.partial(absorb_kernel, plan, kv_local, rows, fac...  11.7 us
    ppermute x5, starting transfers between devices, swapped(): return lax.ppermute(value, axis, [(i, i ^ bit) for i in range(count)])  10.2 us
    ppermute x4, starting transfers between devices, passed_on(): return lax.ppermute(value, 'ctx', pairs)  6.02 us
    ppermute x4, waiting for transfers between devices, passed_on(): return lax.ppermute(value, 'ctx', pairs)  5.14 us
    ppermute x5, waiting for transfers between devices, swapped(): return lax.ppermute(value, axis, [(i, i ^ bit) for i in range(count)])  1.12 us
    pallas_call x1, Pallas kernels, shards(): pl.pallas_call(functools.partial(choose_kernel, kv_local), out_shape=jax....  1 us
    concatenate x1, other arithmetic, shards(): v1 = passed_on(jnp.concatenate([v0, ids]), 1)  0.94 us
  transfers between devices with their start and end apart: 9, of which 3 were waited for; matrix products, arithmetic and copies ran while one was open for 0% of the time, Pallas kernels for 28%

profile of v2, /device:TPU:0, one launch (start us, length us, event | category | flops | bytes accessed | tf_op | source)
XLA Modules:
  0.0 36.8 jit_solution(13423861518417275403)
XLA Ops:
  0.0 0.7 %fusion = bf16[3,128]{1,0:T(4,128)(2,1)S(1)} fusion(s32[384]{0:T(512)} %param.11), kind=kLoop, calls=%fused_computation.2 | loop fusion | flops 768 | bytes 2304 | tf_op jit(solution)/shard_map/reshape | solution.py:350
  0.7 0.9 %pad_maximum_fusion = bf16[784,128]{1,0:T(8,128)(2,1)S(1)} fusion(bf16[16,128]{1,0:T(8,128)(2,1)S(1)} %pad.4.refs_1_, bf16[768,128]{1,0:T(8,128)(2,1)} %bitcast.8), kind=kLoop, calls=%fused_computation | loop fusion | flops 401408 | bytes 401408 | tf_op jit(solution)/shard_map/concatenate | solution.py:353
  1.6 3.1 %collective-permute-start.1 = (bf16[784,128]{1,0:T(8,128)(2,1)S(1)}, bf16[784,128]{1,0:T(8,128)(2,1)S(1)}, u32[]{:S(2)}, u32[]{:S(2)}) collective-permute-start(bf16[784,128]{1,0:T(8,128)(2,1)S(1)} %pad_maximum_fusion), channel_id=1, source_target_pairs={{0,4},{4,8},{8,12},{12,0},{1,5},{5,9},{9,13},{13,1},{2,6},{6,10},{... | collective-permute-start | bytes 602120 | tf_op jit(solution)/shard_map/ppermute | solution.py:29
  4.7 1.6 %collective-permute-start = (bf16[768,128]{1,0:T(8,128)(2,1)}, bf16[768,128]{1,0:T(8,128)(2,1)S(1)}, u32[]{:S(2)}, u32[]{:S(2)}) collective-permute-start(bf16[768,128]{1,0:T(8,128)(2,1)} %bitcast.15), channel_id=1, source_target_pairs={{0,4},{4,8},{8,12},{12,0},{1,5},{5,9},{9,13},{13,1},{2,6},{6,10},{... | collective-permute-start | bytes 589832 | tf_op jit(solution)/shard_map/ppermute | solution.py:29
  6.3 0.0 collective-permute-start.2
  6.3 0.5 %collective-permute-start.3 = (bf16[256,128]{1,0:T(8,128)(2,1)}, bf16[256,128]{1,0:T(8,128)(2,1)S(1)}, u32[]{:S(2)}, u32[]{:S(2)}) collective-permute-start(bf16[256,128]{1,0:T(8,128)(2,1)} %bitcast.12), channel_id=1, source_target_pairs={{0,1},{1,0},{2,3},{3,2},{4,5},{5,4},{6,7},{7,6},{8,9},{9,8},{10,11... | collective-permute-start | bytes 196616 | tf_op jit(solution)/shard_map/ppermute | solution.py:34
  6.8 1.0 %collective-permute-done.2.other_k = bf16[256,128]{1,0:T(8,128)(2,1)S(1)} collective-permute-done((bf16[256,128]{1,0:T(8,128)(2,1)}, bf16[256,128]{1,0:T(8,128)(2,1)S(1)}, u32[]{:S(2)}, u32[]{:S(2)}) %collective-permute-start.2) | collective-permute-done | bytes 65568 | tf_op jit(solution)/shard_map/ppermute | solution.py:34
  7.8 0.2 collective-permute-done.3.other_v
  7.9 1.0 %choose.1.refs_6_ = bf16[512,128]{1,0:T(8,128)(2,1)S(1)} custom-call(bf16[256,128]{1,0:T(8,128)(2,1)} %bitcast.11, bf16[256,128]{1,0:T(8,128)(2,1)} %bitcast.13, bf16[256,128]{1,0:T(8,128)(2,1)S(1)} %collective-permute-done.2.other_k, bf16[256,128]{1,0:T(8,128)(2,1)S(1)} %collective-permute-done.3.other_v), custom_call_target="tpu_custom_call" | custom-call | bytes 262144 | tf_op jit(solution)/shard_map/choose/pallas_call | solution.py:359
  9.0 1.1 %collective-permute-start.4 = (bf16[512,128]{1,0:T(8,128)(2,1)S(1)}, bf16[512,128]{1,0:T(8,128)(2,1)S(1)}, u32[]{:S(2)}, u32[]{:S(2)}) collective-permute-start(bf16[512,128]{1,0:T(8,128)(2,1)S(1)} %choose.1.refs_6_), channel_id=1, source_target_pairs={{0,8},{4,12},{8,0},{12,4},{1,9},{5,13},{9,1},{13,5},{2,10},{6,14},... | collective-permute-start | bytes 393224 | tf_op jit(solution)/shard_map/ppermute | solution.py:34
  10.1 1.7 %collective-permute-start.5 = (bf16[512,128]{1,0:T(8,128)(2,1)S(1)}, bf16[512,128]{1,0:T(8,128)(2,1)S(1)}, u32[]{:S(2)}, u32[]{:S(2)}) collective-permute-start(bf16[512,128]{1,0:T(8,128)(2,1)S(1)} %choose.1.refs_6_), channel_id=1, source_target_pairs={{0,4},{4,0},{8,12},{12,8},{1,5},{5,1},{9,13},{13,9},{2,6},{6,2},{1... | collective-permute-start | bytes 393224 | tf_op jit(solution)/shard_map/ppermute | solution.py:34
  11.8 5.1 %collective-permute-done.refs_4_ = bf16[768,128]{1,0:T(8,128)(2,1)S(1)} collective-permute-done((bf16[768,128]{1,0:T(8,128)(2,1)}, bf16[768,128]{1,0:T(8,128)(2,1)S(1)}, u32[]{:S(2)}, u32[]{:S(2)}) %collective-permute-start) | collective-permute-done | bytes 196640 | tf_op jit(solution)/shard_map/ppermute | solution.py:29
  17.0 0.7 %collective-permute-start.6 = (bf16[768,128]{1,0:T(8,128)(2,1)S(1)}, bf16[768,128]{1,0:T(8,128)(2,1)S(1)}, u32[]{:S(2)}, u32[]{:S(2)}) collective-permute-start(bf16[768,128]{1,0:T(8,128)(2,1)S(1)} %collective-permute-done.refs_4_), channel_id=1, source_target_pairs={{4,8},{8,12},{5,9},{9,13},{6,10},{10,14},{7,11},{11,15},{20,24},{2... | collective-permute-start | bytes 589832 | tf_op jit(solution)/shard_map/ppermute | solution.py:29
  17.6 0.0 collective-permute-done.1.refs_5_
  17.6 0.7 %collective-permute-start.7 = (bf16[784,128]{1,0:T(8,128)(2,1)S(1)}, bf16[784,128]{1,0:T(8,128)(2,1)S(1)}, u32[]{:S(2)}, u32[]{:S(2)}) collective-permute-start(bf16[784,128]{1,0:T(8,128)(2,1)S(1)} %collective-permute-done.1.refs_5_), channel_id=1, source_target_pairs={{4,8},{8,12},{5,9},{9,13},{6,10},{10,14},{7,11},{11,15},{20,24},{2... | collective-permute-start | bytes 602120 | tf_op jit(solution)/shard_map/ppermute | solution.py:29
  18.3 4.1 %shard_map.64 = (f32[10,384,256]{2,1,0:T(8,128)S(1)}, f32[10,384,128]{2,1,0:T(8,128)S(1)}, bf16[10,384,128]{2,1,0:T(8,128)(2,1)S(1)}) custom-call(bf16[10,384,128]{2,1,0:T(8,128)(2,1)} %bitcast.14, bf16[16,128]{1,0:T(8,128)(2,1)S(1)} %pad.4.refs_1_, bf16[768,128]{1,0:T(8,128)(2,1)} %bitcast.16, bf16[768,128]{1,0:T(8,128)(2,1)} %bitcast.9), custom_call_target="tpu_custom_call" | custom-call | flops 754974720 | bytes 4194304 | tf_op jit(solution)/shard_map/pallas_call | solution.py:310
  22.4 0.0 collective-permute-done.4.refs_7_
  22.4 6.8 %collective-permute-start.8 = (bf16[512,128]{1,0:T(8,128)(2,1)S(1)}, bf16[512,128]{1,0:T(8,128)(2,1)S(1)}, u32[]{:S(2)}, u32[]{:S(2)}) collective-permute-start(bf16[512,128]{1,0:T(8,128)(2,1)S(1)} %collective-permute-done.4.refs_7_), channel_id=1, source_target_pairs={{0,4},{4,0},{8,12},{12,8},{1,5},{5,1},{9,13},{13,9},{2,6},{6,2},{1... | collective-permute-start | bytes 393224 | tf_op jit(solution)/shard_map/ppermute | solution.py:34
  29.2 0.0 collective-permute-done.5.refs_8_
  29.2 5.0 %shard_map.65 = (f32[10,384,256]{2,1,0:T(8,128)S(1)}, f32[10,384,128]{2,1,0:T(8,128)S(1)}) custom-call(bf16[10,384,128]{2,1,0:T(8,128)(2,1)S(1)} %get-tuple-element.12.refs_0_, bf16[16,128]{1,0:T(8,128)(2,1)S(1)} %pad.4.refs_1_, f32[10,384,256]{2,1,0:T(8,128)S(1)} %get-tuple-element.13.refs_2_, f32[10,384,128]{2,1,0:T(8,128)S(1)} %get-tuple-element.14.refs_3_, ...), custom_call_target="tpu_custom_call" | custom-call | flops 1509949440 | bytes 4194304 | tf_op jit(solution)/shard_map/pallas_call | solution.py:310
  34.2 0.0 collective-permute-done.6.refs_4_
  34.2 0.0 collective-permute-done.7.refs_5_
  34.2 0.2 shard_map.66
  34.4 0.0 collective-permute-done.8.refs_4_
  34.4 2.4 %shard_map.67 = bf16[10,384,128]{2,1,0:T(8,128)(2,1)} custom-call(bf16[10,384,128]{2,1,0:T(8,128)(2,1)S(1)} %get-tuple-element.12.refs_0_, bf16[16,128]{1,0:T(8,128)(2,1)S(1)} %pad.4.refs_1_, f32[10,384,256]{2,1,0:T(8,128)S(1)} %get-tuple-element.17.refs_2_, f32[10,384,128]{2,1,0:T(8,128)S(1)} %get-tuple-element.18.refs_3_, ...), custom_call_target="tpu_custom_call" | custom-call | flops 251658240 | bytes 4194304 | tf_op jit(solution)/shard_map/pallas_call | solution.py:310
  (1 shorter events, 0.0 us)
Async XLA Ops:
  1.6 16.0 %collective-permute-start.1 = (bf16[784,128]{1,0:T(8,128)(2,1)S(1)}, bf16[784,128]{1,0:T(8,128)(2,1)S(1)}, u32[]{:S(2)}, u32[]{:S(2)}) collective-permute-start(bf16[784,128]{1,0:T(8,128)(2,1)S(1)} %pad_maximum_fusion), channel_id=1, source_target_pairs={{0,4},{4,8},{8,12},{12,0},{1,5},{5,9},{9,13},{13,1},{2,6},{6,10},{... | collective-permute-start | bytes 602120 | tf_op jit(solution)/shard_map/ppermute | solution.py:29
  4.7 12.2 %collective-permute-start = (bf16[768,128]{1,0:T(8,128)(2,1)}, bf16[768,128]{1,0:T(8,128)(2,1)S(1)}, u32[]{:S(2)}, u32[]{:S(2)}) collective-permute-start(bf16[768,128]{1,0:T(8,128)(2,1)} %bitcast.15), channel_id=1, source_target_pairs={{0,4},{4,8},{8,12},{12,0},{1,5},{5,9},{9,13},{13,1},{2,6},{6,10},{... | collective-permute-start | bytes 589832 | tf_op jit(solution)/shard_map/ppermute | solution.py:29
  6.3 1.5 %collective-permute-start.2 = (bf16[256,128]{1,0:T(8,128)(2,1)}, bf16[256,128]{1,0:T(8,128)(2,1)S(1)}, u32[]{:S(2)}, u32[]{:S(2)}) collective-permute-start(bf16[256,128]{1,0:T(8,128)(2,1)} %bitcast.10), channel_id=1, source_target_pairs={{0,1},{1,0},{2,3},{3,2},{4,5},{5,4},{6,7},{7,6},{8,9},{9,8},{10,11... | collective-permute-start | bytes 196616 | tf_op jit(solution)/shard_map/ppermute | solution.py:34
  6.3 1.6 %collective-permute-start.3 = (bf16[256,128]{1,0:T(8,128)(2,1)}, bf16[256,128]{1,0:T(8,128)(2,1)S(1)}, u32[]{:S(2)}, u32[]{:S(2)}) collective-permute-start(bf16[256,128]{1,0:T(8,128)(2,1)} %bitcast.12), channel_id=1, source_target_pairs={{0,1},{1,0},{2,3},{3,2},{4,5},{5,4},{6,7},{7,6},{8,9},{9,8},{10,11... | collective-permute-start | bytes 196616 | tf_op jit(solution)/shard_map/ppermute | solution.py:34
  9.0 13.5 %collective-permute-start.4 = (bf16[512,128]{1,0:T(8,128)(2,1)S(1)}, bf16[512,128]{1,0:T(8,128)(2,1)S(1)}, u32[]{:S(2)}, u32[]{:S(2)}) collective-permute-start(bf16[512,128]{1,0:T(8,128)(2,1)S(1)} %choose.1.refs_6_), channel_id=1, source_target_pairs={{0,8},{4,12},{8,0},{12,4},{1,9},{5,13},{9,1},{13,5},{2,10},{6,14},... | collective-permute-start | bytes 393224 | tf_op jit(solution)/shard_map/ppermute | solution.py:34
  10.1 19.1 %collective-permute-start.5 = (bf16[512,128]{1,0:T(8,128)(2,1)S(1)}, bf16[512,128]{1,0:T(8,128)(2,1)S(1)}, u32[]{:S(2)}, u32[]{:S(2)}) collective-permute-start(bf16[512,128]{1,0:T(8,128)(2,1)S(1)} %choose.1.refs_6_), channel_id=1, source_target_pairs={{0,4},{4,0},{8,12},{12,8},{1,5},{5,1},{9,13},{13,9},{2,6},{6,2},{1... | collective-permute-start | bytes 393224 | tf_op jit(solution)/shard_map/ppermute | solution.py:34
  17.0 17.3 %collective-permute-start.6 = (bf16[768,128]{1,0:T(8,128)(2,1)S(1)}, bf16[768,128]{1,0:T(8,128)(2,1)S(1)}, u32[]{:S(2)}, u32[]{:S(2)}) collective-permute-start(bf16[768,128]{1,0:T(8,128)(2,1)S(1)} %collective-permute-done.refs_4_), channel_id=1, source_target_pairs={{4,8},{8,12},{5,9},{9,13},{6,10},{10,14},{7,11},{11,15},{20,24},{2... | collective-permute-start | bytes 589832 | tf_op jit(solution)/shard_map/ppermute | solution.py:29
  17.6 16.6 %collective-permute-start.7 = (bf16[784,128]{1,0:T(8,128)(2,1)S(1)}, bf16[784,128]{1,0:T(8,128)(2,1)S(1)}, u32[]{:S(2)}, u32[]{:S(2)}) collective-permute-start(bf16[784,128]{1,0:T(8,128)(2,1)S(1)} %collective-permute-done.1.refs_5_), channel_id=1, source_target_pairs={{4,8},{8,12},{5,9},{9,13},{6,10},{10,14},{7,11},{11,15},{20,24},{2... | collective-permute-start | bytes 602120 | tf_op jit(solution)/shard_map/ppermute | solution.py:29
  22.4 12.0 %collective-permute-start.8 = (bf16[512,128]{1,0:T(8,128)(2,1)S(1)}, bf16[512,128]{1,0:T(8,128)(2,1)S(1)}, u32[]{:S(2)}, u32[]{:S(2)}) collective-permute-start(bf16[512,128]{1,0:T(8,128)(2,1)S(1)} %collective-permute-done.4.refs_7_), channel_id=1, source_target_pairs={{0,4},{4,0},{8,12},{12,8},{1,5},{5,1},{9,13},{13,9},{2,6},{6,2},{1... | collective-permute-start | bytes 393224 | tf_op jit(solution)/shard_map/ppermute | solution.py:34

commit v3 on v2

--- a/solution.py
+++ b/solution.py
@@ -89,24 +89,36 @@
 
 
 def attend(
-    q, keys, vals, masked, bias, factor, old, keep, emit, unroll, scores, peaks, tops, weights
+    q, keys, vals, raw, spans, masked, bias, factor, old, keep, emit, unroll, scores, peaks, tops, weights
 ):
     qheads, rows, _ = q.shape
-    blocks = keys.shape[1]
+    blocks = len(spans)
     group = qheads // keys.shape[0]
+
+    for j, (low, high) in enumerate(spans):
+        for first, end in ((0, low), (high, rows)):
+            if first < end:
+                weights[:, j, first:end, :] = jnp.zeros((2, end - first, TILE), BF16)
 
     def score(head, slot):
         kv = head // group
-        wall = jnp.concatenate([keys[kv, j] for j in range(blocks)], axis=1)
-        found = jnp.dot(q[head], wall, preferred_element_type=F32)
-        peak = None
-        for j in range(blocks):
-            piece = found[:, j * TILE : (j + 1) * TILE]
-            if j < masked:
-                piece = piece + bias[j]
-            scores[slot, j] = piece
-            peak = piece if peak is None else jnp.maximum(peak, piece)
-        peaks[slot] = peak
+        if raw is None:
+            wall = jnp.concatenate([keys[kv, j] for j in range(blocks)], axis=1)
+            found = jnp.dot(q[head], wall, preferred_element_type=F32)
+        best = {}
+        for j, (low, high) in enumerate(spans):
+            for first in range(low, high, TILE):
+                part = slice(first, first + TILE)
+                if raw is None:
+                    piece = found[part, j * TILE : (j + 1) * TILE] * factor
+                else:
+                    piece = raw[head, j, part, :]
+                if j < masked:
+                    piece = piece + bias[j, part, :]
+                scores[slot, j, part, :] = piece
+                best[first] = jnp.maximum(best[first], piece) if first in best else piece
+        for first, peak in best.items():
+            peaks[slot, first : first + TILE, :] = peak
 
     def weigh(head, slot):
         for r in range(0, rows, CHUNK):
@@ -119,9 +131,10 @@
                 tops[slot, part, :] = top
             else:
                 keep[head, part, :] = top
-            for j in range(blocks):
-                shifted = (scores[slot, j, part, :] - top) * factor
-                weights[slot, j, part, :] = jnp.exp2(shifted).astype(BF16)
+            for j, (low, high) in enumerate(spans):
+                if low <= r < high:
+                    shifted = scores[slot, j, part, :] - top
+                    weights[slot, j, part, :] = jnp.exp2(shifted).astype(BF16)
 
     def mix(head, slot):
         wall = jnp.concatenate([weights[slot, j] for j in range(blocks)], axis=1)
@@ -152,6 +165,45 @@
     weigh(last, last % 2)
     mix(last - 1, (last - 1) % 2)
     mix(last, last % 2)
+
+
+def ahead_kernel(kv_local, rows, factor, q, k2, out, keys, wide):
+    group = q.shape[0] // kv_local
+    blocks = rows // TILE
+
+    def one_head(head, _):
+        kv = head // group
+        wall = jnp.concatenate([keys[kv, j] for j in range(blocks)], axis=1)
+        found = jnp.dot(q[head], wall, preferred_element_type=F32)
+        for j in range(blocks):
+            high = (j + 1) * TILE
+            out[head, j, 0:high, :] = found[0:high, j * TILE : high] * factor
+        return 0
+
+    @pl.when(lax.axis_index("ctx") >= 2)
+    def _():
+        place_keys(k2, rows, kv_local, wide, keys, 0)
+        lax.fori_loop(0, q.shape[0], one_head, 0, unroll=True)
+
+
+def ahead(queries, k2, kv_local, factor):
+    qheads, rows, width = queries.shape
+    blocks = rows // TILE
+    return pl.pallas_call(
+        functools.partial(ahead_kernel, kv_local, rows, factor),
+        out_shape=jax.ShapeDtypeStruct((qheads, blocks, rows, TILE), F32),
+        in_specs=[VM] * 2,
+        out_specs=VM,
+        scratch_shapes=[
+            pltpu.VMEM((kv_local, blocks, width, TILE), BF16),
+            pltpu.VMEM((rows * kv_local, width), F32),
+        ],
+        cost_estimate=pl.CostEstimate(
+            flops=2 * rows * qheads * rows * width, bytes_accessed=2**20, transcendentals=0
+        ),
+        compiler_params=pltpu.CompilerParams(vmem_limit_bytes=GRANT),
+        name="ahead",
+    )(queries, k2)
 
 
 def absorb_kernel(plan, kv_local, rows, factor, *refs):
@@ -176,8 +228,10 @@
         for move in moves:
             move.start()
         q = landed
+    raw = None
     if plan["skips"]:
         acc, stat = outs
+        raw = sources[0][1][0]
     if final:
         ready, leaving = refs[-2:]
         refs = refs[:-2]
@@ -194,13 +248,19 @@
         mine = ids[...]
         at = 0
         masked = 0
-        places = []
+        places, spans = [], []
         for kind, taken in sources:
             places.append((kind == "own", at, kind, taken))
             if kind == "prefix":
-                at += sum(chunk.shape[0] for chunk in taken) // (2 * kv_local)
+                size = sum(chunk.shape[0] for chunk in taken) // (2 * kv_local)
             else:
-                at += rows
+                size = rows
+            for first in range(0, size, TILE):
+                low = first if kind == "own" else 0
+                high = first + TILE if kind == "back2" else rows
+                spans.append((low, high))
+            at += size
+            if kind != "prefix":
                 masked = at // TILE
         for own, at, kind, taken in sorted(places, key=lambda place: place[:2]):
             if kind == "prefix":
@@ -226,23 +286,24 @@
                 column = id_column(mine, i)
                 part = slice(i * TILE, (i + 1) * TILE)
                 for j in range(tiles):
+                    low, high = spans[at // TILE + j]
+                    if not low <= i * TILE < high:
+                        continue
                     seen = column == id_row(other, j)
                     if kind == "own" and j == i:
                         seen = seen & (place <= spot)
-                    piece = jnp.where(seen, 0.0, HIDDEN)
-                    if kind == "own" and j > i:
-                        piece = jnp.full((TILE, TILE), HIDDEN, F32)
-                    bias[at // TILE + j, part, :] = piece
+                    bias[at // TILE + j, part, :] = jnp.where(seen, 0.0, HIDDEN)
             if own:
                 moves[0].wait()
                 moves[1].wait()
-            place_keys(taken[0], rows, kv_local, wide, keys, at)
+            if not plan["skips"]:
+                place_keys(taken[0], rows, kv_local, wide, keys, at)
             place_values(taken[1], rows, kv_local, wide, vals, at)
 
         def emit(head, top, mixed):
             upper, lower = mixed[:, 0:TILE], mixed[:, TILE:]
             if started:
-                fade = jnp.exp2((stat[head] - top) * factor)
+                fade = jnp.exp2(stat[head] - top)
                 upper = acc[head, :, 0:TILE] * fade + upper
                 lower = acc[head, :, TILE:] * fade + lower
             if final:
@@ -257,7 +318,7 @@
         if not started:
             moves[2].wait()
         keep = None if final or plan["skips"] else outs[1]
-        attend(q, keys, vals, masked, bias, factor, stat, keep, emit, 8 if final else 4, *room)
+        attend(q, keys, vals, raw, spans, masked, bias, factor, stat, keep, emit, 8 if final or plan["skips"] else 4, *room)
 
     if plan["skips"]:
         pl.when(visible_at_all())(work)
@@ -393,7 +454,8 @@
     args = (queries, ids)
     near = [("back1", [k1, v1]), ("prefix", prefix[:-1])]
     state = absorb(near, False, *args, state, *rest)
-    state = absorb([("back2", [k2, v2])], False, *args, state, *rest)
+    raw = ahead(queries, k2, kv_local, factor)
+    state = absorb([("back2", [raw, v2])], False, *args, state, *rest)
     (out,) = absorb([("prefix", prefix[-1:])], True, *args, state, *rest)
     return out.transpose(1, 0, 2)
 

time: 37.1 us -> 37 us (level)
  transfers between devices with their start and end apart: 9 -> 9, of which waited for: 3 -> 3; matrix products, arithmetic and copies ran while one was open for 0% -> 0% of each run, Pallas kernels for 28% -> 27%
where the time goes in v3:
time: 37 us; the launch traced here: 36.8 us
  starting transfers between devices  16.2 us (44%)
  Pallas kernels  12.6 us (34%)
  waiting for transfers between devices  6.26 us (17%)
  other arithmetic  1.63 us (4%)
    pallas_call x4, Pallas kernels, absorb(): pl.pallas_call(functools.partial(absorb_kernel, plan, kv_local, rows, fac...  11.6 us
    ppermute x5, starting transfers between devices, swapped(): return lax.ppermute(value, axis, [(i, i ^ bit) for i in range(count)])  10.2 us
    ppermute x4, starting transfers between devices, passed_on(): return lax.ppermute(value, 'ctx', pairs)  6.02 us
    ppermute x4, waiting for transfers between devices, passed_on(): return lax.ppermute(value, 'ctx', pairs)  5.14 us
    ppermute x5, waiting for transfers between devices, swapped(): return lax.ppermute(value, axis, [(i, i ^ bit) for i in range(count)])  1.12 us
    pallas_call x1, Pallas kernels, shards(): pl.pallas_call(functools.partial(choose_kernel, kv_local), out_shape=jax....  1 us
    concatenate x1, other arithmetic, shards(): v1 = passed_on(jnp.concatenate([v0, ids]), 1)  0.94 us
  transfers between devices with their start and end apart: 9, of which 3 were waited for; matrix products, arithmetic and copies ran while one was open for 0% of the time, Pallas kernels for 27%

profile of v3, /device:TPU:0, one launch (start us, length us, event | category | flops | bytes accessed | tf_op | source)
XLA Modules:
  0.0 36.8 jit_solution(6019665765230452998)
XLA Ops:
  0.0 0.7 %fusion = bf16[3,128]{1,0:T(4,128)(2,1)S(1)} fusion(s32[384]{0:T(512)} %param.11), kind=kLoop, calls=%fused_computation.2 | loop fusion | flops 768 | bytes 2304 | tf_op jit(solution)/shard_map/reshape | solution.py:411
  0.7 0.9 %pad_maximum_fusion = bf16[784,128]{1,0:T(8,128)(2,1)S(1)} fusion(bf16[16,128]{1,0:T(8,128)(2,1)S(1)} %pad.4.refs_1_, bf16[768,128]{1,0:T(8,128)(2,1)} %bitcast.8), kind=kLoop, calls=%fused_computation | loop fusion | flops 401408 | bytes 401408 | tf_op jit(solution)/shard_map/concatenate | solution.py:414
  1.6 3.1 %collective-permute-start.1 = (bf16[784,128]{1,0:T(8,128)(2,1)S(1)}, bf16[784,128]{1,0:T(8,128)(2,1)S(1)}, u32[]{:S(2)}, u32[]{:S(2)}) collective-permute-start(bf16[784,128]{1,0:T(8,128)(2,1)S(1)} %pad_maximum_fusion), channel_id=1, source_target_pairs={{0,4},{4,8},{8,12},{12,0},{1,5},{5,9},{9,13},{13,1},{2,6},{6,10},{... | collective-permute-start | bytes 602120 | tf_op jit(solution)/shard_map/ppermute | solution.py:29
  4.7 1.6 %collective-permute-start = (bf16[768,128]{1,0:T(8,128)(2,1)}, bf16[768,128]{1,0:T(8,128)(2,1)S(1)}, u32[]{:S(2)}, u32[]{:S(2)}) collective-permute-start(bf16[768,128]{1,0:T(8,128)(2,1)} %bitcast.15), channel_id=1, source_target_pairs={{0,4},{4,8},{8,12},{12,0},{1,5},{5,9},{9,13},{13,1},{2,6},{6,10},{... | collective-permute-start | bytes 589832 | tf_op jit(solution)/shard_map/ppermute | solution.py:29
  6.3 0.0 collective-permute-start.2
  6.3 0.5 %collective-permute-start.3 = (bf16[256,128]{1,0:T(8,128)(2,1)}, bf16[256,128]{1,0:T(8,128)(2,1)S(1)}, u32[]{:S(2)}, u32[]{:S(2)}) collective-permute-start(bf16[256,128]{1,0:T(8,128)(2,1)} %bitcast.12), channel_id=1, source_target_pairs={{0,1},{1,0},{2,3},{3,2},{4,5},{5,4},{6,7},{7,6},{8,9},{9,8},{10,11... | collective-permute-start | bytes 196616 | tf_op jit(solution)/shard_map/ppermute | solution.py:34
  6.8 1.0 %collective-permute-done.2.other_k = bf16[256,128]{1,0:T(8,128)(2,1)S(1)} collective-permute-done((bf16[256,128]{1,0:T(8,128)(2,1)}, bf16[256,128]{1,0:T(8,128)(2,1)S(1)}, u32[]{:S(2)}, u32[]{:S(2)}) %collective-permute-start.2) | collective-permute-done | bytes 65568 | tf_op jit(solution)/shard_map/ppermute | solution.py:34
  7.8 0.2 collective-permute-done.3.other_v
  7.9 1.0 %choose.1.refs_6_ = bf16[512,128]{1,0:T(8,128)(2,1)S(1)} custom-call(bf16[256,128]{1,0:T(8,128)(2,1)} %bitcast.11, bf16[256,128]{1,0:T(8,128)(2,1)} %bitcast.13, bf16[256,128]{1,0:T(8,128)(2,1)S(1)} %collective-permute-done.2.other_k, bf16[256,128]{1,0:T(8,128)(2,1)S(1)} %collective-permute-done.3.other_v), custom_call_target="tpu_custom_call" | custom-call | bytes 262144 | tf_op jit(solution)/shard_map/choose/pallas_call | solution.py:420
  9.0 1.1 %collective-permute-start.4 = (bf16[512,128]{1,0:T(8,128)(2,1)S(1)}, bf16[512,128]{1,0:T(8,128)(2,1)S(1)}, u32[]{:S(2)}, u32[]{:S(2)}) collective-permute-start(bf16[512,128]{1,0:T(8,128)(2,1)S(1)} %choose.1.refs_6_), channel_id=1, source_target_pairs={{0,8},{4,12},{8,0},{12,4},{1,9},{5,13},{9,1},{13,5},{2,10},{6,14},... | collective-permute-start | bytes 393224 | tf_op jit(solution)/shard_map/ppermute | solution.py:34
  10.1 1.7 %collective-permute-start.5 = (bf16[512,128]{1,0:T(8,128)(2,1)S(1)}, bf16[512,128]{1,0:T(8,128)(2,1)S(1)}, u32[]{:S(2)}, u32[]{:S(2)}) collective-permute-start(bf16[512,128]{1,0:T(8,128)(2,1)S(1)} %choose.1.refs_6_), channel_id=1, source_target_pairs={{0,4},{4,0},{8,12},{12,8},{1,5},{5,1},{9,13},{13,9},{2,6},{6,2},{1... | collective-permute-start | bytes 393224 | tf_op jit(solution)/shard_map/ppermute | solution.py:34
  11.8 5.1 %collective-permute-done.refs_4_ = bf16[768,128]{1,0:T(8,128)(2,1)S(1)} collective-permute-done((bf16[768,128]{1,0:T(8,128)(2,1)}, bf16[768,128]{1,0:T(8,128)(2,1)S(1)}, u32[]{:S(2)}, u32[]{:S(2)}) %collective-permute-start) | collective-permute-done | bytes 196640 | tf_op jit(solution)/shard_map/ppermute | solution.py:29
  17.0 0.7 %collective-permute-start.6 = (bf16[768,128]{1,0:T(8,128)(2,1)S(1)}, bf16[768,128]{1,0:T(8,128)(2,1)S(1)}, u32[]{:S(2)}, u32[]{:S(2)}) collective-permute-start(bf16[768,128]{1,0:T(8,128)(2,1)S(1)} %collective-permute-done.refs_4_), channel_id=1, source_target_pairs={{4,8},{8,12},{5,9},{9,13},{6,10},{10,14},{7,11},{11,15},{20,24},{2... | collective-permute-start | bytes 589832 | tf_op jit(solution)/shard_map/ppermute | solution.py:29
  17.6 0.0 collective-permute-done.1.refs_5_
  17.6 0.7 %collective-permute-start.7 = (bf16[784,128]{1,0:T(8,128)(2,1)S(1)}, bf16[784,128]{1,0:T(8,128)(2,1)S(1)}, u32[]{:S(2)}, u32[]{:S(2)}) collective-permute-start(bf16[784,128]{1,0:T(8,128)(2,1)S(1)} %collective-permute-done.1.refs_5_), channel_id=1, source_target_pairs={{4,8},{8,12},{5,9},{9,13},{6,10},{10,14},{7,11},{11,15},{20,24},{2... | collective-permute-start | bytes 602120 | tf_op jit(solution)/shard_map/ppermute | solution.py:29
  18.3 4.0 %shard_map.64 = (f32[10,384,256]{2,1,0:T(8,128)S(1)}, f32[10,384,128]{2,1,0:T(8,128)S(1)}, bf16[10,384,128]{2,1,0:T(8,128)(2,1)S(1)}) custom-call(bf16[10,384,128]{2,1,0:T(8,128)(2,1)} %bitcast.14, bf16[16,128]{1,0:T(8,128)(2,1)S(1)} %pad.4.refs_1_, bf16[768,128]{1,0:T(8,128)(2,1)} %bitcast.16, bf16[768,128]{1,0:T(8,128)(2,1)} %bitcast.9), custom_call_target="tpu_custom_call" | custom-call | flops 754974720 | bytes 4194304 | tf_op jit(solution)/shard_map/pallas_call | solution.py:371
  22.3 0.0 collective-permute-done.4.refs_7_
  22.3 6.8 %collective-permute-start.8 = (bf16[512,128]{1,0:T(8,128)(2,1)S(1)}, bf16[512,128]{1,0:T(8,128)(2,1)S(1)}, u32[]{:S(2)}, u32[]{:S(2)}) collective-permute-start(bf16[512,128]{1,0:T(8,128)(2,1)S(1)} %collective-permute-done.4.refs_7_), channel_id=1, source_target_pairs={{0,4},{4,0},{8,12},{12,8},{1,5},{5,1},{9,13},{13,9},{2,6},{6,2},{1... | collective-permute-start | bytes 393224 | tf_op jit(solution)/shard_map/ppermute | solution.py:34
  29.1 0.0 collective-permute-done.5.refs_8_
  29.1 4.8 %shard_map.65 = (f32[10,384,256]{2,1,0:T(8,128)S(1)}, f32[10,384,128]{2,1,0:T(8,128)S(1)}) custom-call(bf16[10,384,128]{2,1,0:T(8,128)(2,1)S(1)} %get-tuple-element.12.refs_0_.q, bf16[16,128]{1,0:T(8,128)(2,1)S(1)} %pad.4.refs_1_, f32[10,384,256]{2,1,0:T(8,128)S(1)} %get-tuple-element.13.refs_2_, f32[10,384,128]{2,1,0:T(8,128)S(1)} %get-tuple-element.14.refs_3_, ...), custom_call_target="tpu_custom_call" | custom-call | flops 1509949440 | bytes 4194304 | tf_op jit(solution)/shard_map/pallas_call | solution.py:371
  34.0 0.0 collective-permute-done.6.k2
  34.0 0.0 collective-permute-done.7.refs_5_
  34.0 0.2 shard_map.66
  34.2 0.0 collective-permute-done.8.refs_4_
  34.2 2.6 %shard_map.67 = bf16[10,384,128]{2,1,0:T(8,128)(2,1)} custom-call(bf16[10,384,128]{2,1,0:T(8,128)(2,1)S(1)} %get-tuple-element.12.refs_0_.q, bf16[16,128]{1,0:T(8,128)(2,1)S(1)} %pad.4.refs_1_, f32[10,384,256]{2,1,0:T(8,128)S(1)} %get-tuple-element.17.refs_2_, f32[10,384,128]{2,1,0:T(8,128)S(1)} %get-tuple-element.18.refs_3_, ...), custom_call_target="tpu_custom_call" | custom-call | flops 251658240 | bytes 4194304 | tf_op jit(solution)/shard_map/pallas_call | solution.py:371
  (2 shorter events, 0.0 us)
Async XLA Ops:
  1.6 16.0 %collective-permute-start.1 = (bf16[784,128]{1,0:T(8,128)(2,1)S(1)}, bf16[784,128]{1,0:T(8,128)(2,1)S(1)}, u32[]{:S(2)}, u32[]{:S(2)}) collective-permute-start(bf16[784,128]{1,0:T(8,128)(2,1)S(1)} %pad_maximum_fusion), channel_id=1, source_target_pairs={{0,4},{4,8},{8,12},{12,0},{1,5},{5,9},{9,13},{13,1},{2,6},{6,10},{... | collective-permute-start | bytes 602120 | tf_op jit(solution)/shard_map/ppermute | solution.py:29
  4.7 12.2 %collective-permute-start = (bf16[768,128]{1,0:T(8,128)(2,1)}, bf16[768,128]{1,0:T(8,128)(2,1)S(1)}, u32[]{:S(2)}, u32[]{:S(2)}) collective-permute-start(bf16[768,128]{1,0:T(8,128)(2,1)} %bitcast.15), channel_id=1, source_target_pairs={{0,4},{4,8},{8,12},{12,0},{1,5},{5,9},{9,13},{13,1},{2,6},{6,10},{... | collective-permute-start | bytes 589832 | tf_op jit(solution)/shard_map/ppermute | solution.py:29
  6.3 1.5 %collective-permute-start.2 = (bf16[256,128]{1,0:T(8,128)(2,1)}, bf16[256,128]{1,0:T(8,128)(2,1)S(1)}, u32[]{:S(2)}, u32[]{:S(2)}) collective-permute-start(bf16[256,128]{1,0:T(8,128)(2,1)} %bitcast.10), channel_id=1, source_target_pairs={{0,1},{1,0},{2,3},{3,2},{4,5},{5,4},{6,7},{7,6},{8,9},{9,8},{10,11... | collective-permute-start | bytes 196616 | tf_op jit(solution)/shard_map/ppermute | solution.py:34
  6.3 1.6 %collective-permute-start.3 = (bf16[256,128]{1,0:T(8,128)(2,1)}, bf16[256,128]{1,0:T(8,128)(2,1)S(1)}, u32[]{:S(2)}, u32[]{:S(2)}) collective-permute-start(bf16[256,128]{1,0:T(8,128)(2,1)} %bitcast.12), channel_id=1, source_target_pairs={{0,1},{1,0},{2,3},{3,2},{4,5},{5,4},{6,7},{7,6},{8,9},{9,8},{10,11... | collective-permute-start | bytes 196616 | tf_op jit(solution)/shard_map/ppermute | solution.py:34
  9.0 13.3 %collective-permute-start.4 = (bf16[512,128]{1,0:T(8,128)(2,1)S(1)}, bf16[512,128]{1,0:T(8,128)(2,1)S(1)}, u32[]{:S(2)}, u32[]{:S(2)}) collective-permute-start(bf16[512,128]{1,0:T(8,128)(2,1)S(1)} %choose.1.refs_6_), channel_id=1, source_target_pairs={{0,8},{4,12},{8,0},{12,4},{1,9},{5,13},{9,1},{13,5},{2,10},{6,14},... | collective-permute-start | bytes 393224 | tf_op jit(solution)/shard_map/ppermute | solution.py:34
  10.1 19.0 %collective-permute-start.5 = (bf16[512,128]{1,0:T(8,128)(2,1)S(1)}, bf16[512,128]{1,0:T(8,128)(2,1)S(1)}, u32[]{:S(2)}, u32[]{:S(2)}) collective-permute-start(bf16[512,128]{1,0:T(8,128)(2,1)S(1)} %choose.1.refs_6_), channel_id=1, source_target_pairs={{0,4},{4,0},{8,12},{12,8},{1,5},{5,1},{9,13},{13,9},{2,6},{6,2},{1... | collective-permute-start | bytes 393224 | tf_op jit(solution)/shard_map/ppermute | solution.py:34
  17.0 17.0 %collective-permute-start.6 = (bf16[768,128]{1,0:T(8,128)(2,1)S(1)}, bf16[768,128]{1,0:T(8,128)(2,1)S(1)}, u32[]{:S(2)}, u32[]{:S(2)}) collective-permute-start(bf16[768,128]{1,0:T(8,128)(2,1)S(1)} %collective-permute-done.refs_4_), channel_id=1, source_target_pairs={{4,8},{8,12},{5,9},{9,13},{6,10},{10,14},{7,11},{11,15},{20,24},{2... | collective-permute-start | bytes 589832 | tf_op jit(solution)/shard_map/ppermute | solution.py:29
  17.6 16.3 %collective-permute-start.7 = (bf16[784,128]{1,0:T(8,128)(2,1)S(1)}, bf16[784,128]{1,0:T(8,128)(2,1)S(1)}, u32[]{:S(2)}, u32[]{:S(2)}) collective-permute-start(bf16[784,128]{1,0:T(8,128)(2,1)S(1)} %collective-permute-done.1.refs_5_), channel_id=1, source_target_pairs={{4,8},{8,12},{5,9},{9,13},{6,10},{10,14},{7,11},{11,15},{20,24},{2... | collective-permute-start | bytes 602120 | tf_op jit(solution)/shard_map/ppermute | solution.py:29
  22.3 11.9 %collective-permute-start.8 = (bf16[512,128]{1,0:T(8,128)(2,1)S(1)}, bf16[512,128]{1,0:T(8,128)(2,1)S(1)}, u32[]{:S(2)}, u32[]{:S(2)}) collective-permute-start(bf16[512,128]{1,0:T(8,128)(2,1)S(1)} %collective-permute-done.4.refs_7_), channel_id=1, source_target_pairs={{0,4},{4,0},{8,12},{12,8},{1,5},{5,1},{9,13},{13,9},{2,6},{6,2},{1... | collective-permute-start | bytes 393224 | tf_op jit(solution)/shard_map/ppermute | solution.py:34

commit v4 on v3

--- a/solution.py
+++ b/solution.py
@@ -93,6 +93,7 @@
 ):
     qheads, rows, _ = q.shape
     blocks = len(spans)
+    plain = masked == 0
     group = qheads // keys.shape[0]
 
     for j, (low, high) in enumerate(spans):
@@ -110,7 +111,8 @@
             for first in range(low, high, TILE):
                 part = slice(first, first + TILE)
                 if raw is None:
-                    piece = found[part, j * TILE : (j + 1) * TILE] * factor
+                    piece = found[part, j * TILE : (j + 1) * TILE]
+                    piece = piece if plain else piece * factor
                 else:
                     piece = raw[head, j, part, :]
                 if j < masked:
@@ -125,6 +127,7 @@
             part = slice(r, r + CHUNK)
             top = jnp.max(peaks[slot, part, :], axis=1, keepdims=True)
             top = jnp.broadcast_to(top, (CHUNK, TILE))
+            top = top * factor if plain else top
             if old is not None:
                 top = jnp.maximum(top, old[head, part, :])
             if keep is None:
@@ -133,7 +136,8 @@
                 keep[head, part, :] = top
             for j, (low, high) in enumerate(spans):
                 if low <= r < high:
-                    shifted = scores[slot, j, part, :] - top
+                    value = scores[slot, j, part, :]
+                    shifted = (value * factor if plain else value) - top
                     weights[slot, j, part, :] = jnp.exp2(shifted).astype(BF16)
 
     def mix(head, slot):
@@ -318,7 +322,7 @@
         if not started:
             moves[2].wait()
         keep = None if final or plan["skips"] else outs[1]
-        attend(q, keys, vals, raw, spans, masked, bias, factor, stat, keep, emit, 8 if final or plan["skips"] else 4, *room)
+        attend(q, keys, vals, raw, spans, masked, bias, factor, stat, keep, emit, 8, *room)
 
     if plan["skips"]:
         pl.when(visible_at_all())(work)

time: 37 us -> 36.8 us (level)
  no operation moved by 1% of the time
where the time goes in v4:
time: 36.8 us; the launch traced here: 36.5 us
  starting transfers between devices  16.2 us (44%)
  Pallas kernels  12.3 us (33%)
  waiting for transfers between devices  6.26 us (17%)
  other arithmetic  1.63 us (4%)
    pallas_call x4, Pallas kernels, absorb(): pl.pallas_call(functools.partial(absorb_kernel, plan, kv_local, rows, fac...  11.3 us
    ppermute x5, starting transfers between devices, swapped(): return lax.ppermute(value, axis, [(i, i ^ bit) for i in range(count)])  10.2 us
    ppermute x4, starting transfers between devices, passed_on(): return lax.ppermute(value, 'ctx', pairs)  6.02 us
    ppermute x4, waiting for transfers between devices, passed_on(): return lax.ppermute(value, 'ctx', pairs)  5.14 us
    ppermute x5, waiting for transfers between devices, swapped(): return lax.ppermute(value, axis, [(i, i ^ bit) for i in range(count)])  1.12 us
    pallas_call x1, Pallas kernels, shards(): pl.pallas_call(functools.partial(choose_kernel, kv_local), out_shape=jax....  1 us
    concatenate x1, other arithmetic, shards(): v1 = passed_on(jnp.concatenate([v0, ids]), 1)  0.94 us
  transfers between devices with their start and end apart: 9, of which 3 were waited for; matrix products, arithmetic and copies ran while one was open for 0% of the time, Pallas kernels for 27%

profile of v4, /device:TPU:0, one launch (start us, length us, event | category | flops | bytes accessed | tf_op | source)
XLA Modules:
  0.0 36.5 jit_solution(3394475288799100243)
XLA Ops:
  0.0 0.7 %fusion = bf16[3,128]{1,0:T(4,128)(2,1)S(1)} fusion(s32[384]{0:T(512)} %param.11), kind=kLoop, calls=%fused_computation.2 | loop fusion | flops 768 | bytes 2304 | tf_op jit(solution)/shard_map/reshape | solution.py:415
  0.7 0.9 %pad_maximum_fusion = bf16[784,128]{1,0:T(8,128)(2,1)S(1)} fusion(bf16[16,128]{1,0:T(8,128)(2,1)S(1)} %pad.4.refs_1_, bf16[768,128]{1,0:T(8,128)(2,1)} %bitcast.8), kind=kLoop, calls=%fused_computation | loop fusion | flops 401408 | bytes 401408 | tf_op jit(solution)/shard_map/concatenate | solution.py:418
  1.6 3.1 %collective-permute-start.1 = (bf16[784,128]{1,0:T(8,128)(2,1)S(1)}, bf16[784,128]{1,0:T(8,128)(2,1)S(1)}, u32[]{:S(2)}, u32[]{:S(2)}) collective-permute-start(bf16[784,128]{1,0:T(8,128)(2,1)S(1)} %pad_maximum_fusion), channel_id=1, source_target_pairs={{0,4},{4,8},{8,12},{12,0},{1,5},{5,9},{9,13},{13,1},{2,6},{6,10},{... | collective-permute-start | bytes 602120 | tf_op jit(solution)/shard_map/ppermute | solution.py:29
  4.7 1.6 %collective-permute-start = (bf16[768,128]{1,0:T(8,128)(2,1)}, bf16[768,128]{1,0:T(8,128)(2,1)S(1)}, u32[]{:S(2)}, u32[]{:S(2)}) collective-permute-start(bf16[768,128]{1,0:T(8,128)(2,1)} %bitcast.15), channel_id=1, source_target_pairs={{0,4},{4,8},{8,12},{12,0},{1,5},{5,9},{9,13},{13,1},{2,6},{6,10},{... | collective-permute-start | bytes 589832 | tf_op jit(solution)/shard_map/ppermute | solution.py:29
  6.3 0.0 collective-permute-start.2
  6.3 0.5 %collective-permute-start.3 = (bf16[256,128]{1,0:T(8,128)(2,1)}, bf16[256,128]{1,0:T(8,128)(2,1)S(1)}, u32[]{:S(2)}, u32[]{:S(2)}) collective-permute-start(bf16[256,128]{1,0:T(8,128)(2,1)} %bitcast.12), channel_id=1, source_target_pairs={{0,1},{1,0},{2,3},{3,2},{4,5},{5,4},{6,7},{7,6},{8,9},{9,8},{10,11... | collective-permute-start | bytes 196616 | tf_op jit(solution)/shard_map/ppermute | solution.py:34
  6.8 1.0 %collective-permute-done.2.other_k = bf16[256,128]{1,0:T(8,128)(2,1)S(1)} collective-permute-done((bf16[256,128]{1,0:T(8,128)(2,1)}, bf16[256,128]{1,0:T(8,128)(2,1)S(1)}, u32[]{:S(2)}, u32[]{:S(2)}) %collective-permute-start.2) | collective-permute-done | bytes 65568 | tf_op jit(solution)/shard_map/ppermute | solution.py:34
  7.8 0.2 collective-permute-done.3.other_v
  7.9 1.0 %choose.1.refs_6_ = bf16[512,128]{1,0:T(8,128)(2,1)S(1)} custom-call(bf16[256,128]{1,0:T(8,128)(2,1)} %bitcast.11, bf16[256,128]{1,0:T(8,128)(2,1)} %bitcast.13, bf16[256,128]{1,0:T(8,128)(2,1)S(1)} %collective-permute-done.2.other_k, bf16[256,128]{1,0:T(8,128)(2,1)S(1)} %collective-permute-done.3.other_v), custom_call_target="tpu_custom_call" | custom-call | bytes 262144 | tf_op jit(solution)/shard_map/choose/pallas_call | solution.py:424
  9.0 1.1 %collective-permute-start.4 = (bf16[512,128]{1,0:T(8,128)(2,1)S(1)}, bf16[512,128]{1,0:T(8,128)(2,1)S(1)}, u32[]{:S(2)}, u32[]{:S(2)}) collective-permute-start(bf16[512,128]{1,0:T(8,128)(2,1)S(1)} %choose.1.refs_6_), channel_id=1, source_target_pairs={{0,8},{4,12},{8,0},{12,4},{1,9},{5,13},{9,1},{13,5},{2,10},{6,14},... | collective-permute-start | bytes 393224 | tf_op jit(solution)/shard_map/ppermute | solution.py:34
  10.1 1.7 %collective-permute-start.5 = (bf16[512,128]{1,0:T(8,128)(2,1)S(1)}, bf16[512,128]{1,0:T(8,128)(2,1)S(1)}, u32[]{:S(2)}, u32[]{:S(2)}) collective-permute-start(bf16[512,128]{1,0:T(8,128)(2,1)S(1)} %choose.1.refs_6_), channel_id=1, source_target_pairs={{0,4},{4,0},{8,12},{12,8},{1,5},{5,1},{9,13},{13,9},{2,6},{6,2},{1... | collective-permute-start | bytes 393224 | tf_op jit(solution)/shard_map/ppermute | solution.py:34
  11.8 5.1 %collective-permute-done.refs_4_ = bf16[768,128]{1,0:T(8,128)(2,1)S(1)} collective-permute-done((bf16[768,128]{1,0:T(8,128)(2,1)}, bf16[768,128]{1,0:T(8,128)(2,1)S(1)}, u32[]{:S(2)}, u32[]{:S(2)}) %collective-permute-start) | collective-permute-done | bytes 196640 | tf_op jit(solution)/shard_map/ppermute | solution.py:29
  17.0 0.7 %collective-permute-start.6 = (bf16[768,128]{1,0:T(8,128)(2,1)S(1)}, bf16[768,128]{1,0:T(8,128)(2,1)S(1)}, u32[]{:S(2)}, u32[]{:S(2)}) collective-permute-start(bf16[768,128]{1,0:T(8,128)(2,1)S(1)} %collective-permute-done.refs_4_), channel_id=1, source_target_pairs={{4,8},{8,12},{5,9},{9,13},{6,10},{10,14},{7,11},{11,15},{20,24},{2... | collective-permute-start | bytes 589832 | tf_op jit(solution)/shard_map/ppermute | solution.py:29
  17.6 0.0 collective-permute-done.1.refs_5_
  17.6 0.7 %collective-permute-start.7 = (bf16[784,128]{1,0:T(8,128)(2,1)S(1)}, bf16[784,128]{1,0:T(8,128)(2,1)S(1)}, u32[]{:S(2)}, u32[]{:S(2)}) collective-permute-start(bf16[784,128]{1,0:T(8,128)(2,1)S(1)} %collective-permute-done.1.refs_5_), channel_id=1, source_target_pairs={{4,8},{8,12},{5,9},{9,13},{6,10},{10,14},{7,11},{11,15},{20,24},{2... | collective-permute-start | bytes 602120 | tf_op jit(solution)/shard_map/ppermute | solution.py:29
  18.3 3.6 %shard_map.64 = (f32[10,384,256]{2,1,0:T(8,128)S(1)}, f32[10,384,128]{2,1,0:T(8,128)S(1)}, bf16[10,384,128]{2,1,0:T(8,128)(2,1)S(1)}) custom-call(bf16[10,384,128]{2,1,0:T(8,128)(2,1)} %bitcast.14, bf16[16,128]{1,0:T(8,128)(2,1)S(1)} %pad.4.refs_1_, bf16[768,128]{1,0:T(8,128)(2,1)} %bitcast.16, bf16[768,128]{1,0:T(8,128)(2,1)} %bitcast.9), custom_call_target="tpu_custom_call" | custom-call | flops 754974720 | bytes 4194304 | tf_op jit(solution)/shard_map/pallas_call | solution.py:375
  21.9 0.0 collective-permute-done.4.refs_7_
  21.9 6.8 %collective-permute-start.8 = (bf16[512,128]{1,0:T(8,128)(2,1)S(1)}, bf16[512,128]{1,0:T(8,128)(2,1)S(1)}, u32[]{:S(2)}, u32[]{:S(2)}) collective-permute-start(bf16[512,128]{1,0:T(8,128)(2,1)S(1)} %collective-permute-done.4.refs_7_), channel_id=1, source_target_pairs={{0,4},{4,0},{8,12},{12,8},{1,5},{5,1},{9,13},{13,9},{2,6},{6,2},{1... | collective-permute-start | bytes 393224 | tf_op jit(solution)/shard_map/ppermute | solution.py:34
  28.7 0.0 collective-permute-done.5.refs_8_
  28.7 5.0 %shard_map.65 = (f32[10,384,256]{2,1,0:T(8,128)S(1)}, f32[10,384,128]{2,1,0:T(8,128)S(1)}) custom-call(bf16[10,384,128]{2,1,0:T(8,128)(2,1)S(1)} %get-tuple-element.12.refs_0_.q, bf16[16,128]{1,0:T(8,128)(2,1)S(1)} %pad.4.refs_1_, f32[10,384,256]{2,1,0:T(8,128)S(1)} %get-tuple-element.13.refs_2_, f32[10,384,128]{2,1,0:T(8,128)S(1)} %get-tuple-element.14.refs_3_, ...), custom_call_target="tpu_custom_call" | custom-call | flops 1509949440 | bytes 4194304 | tf_op jit(solution)/shard_map/pallas_call | solution.py:375
  33.8 0.0 collective-permute-done.6.k2
  33.8 0.0 collective-permute-done.7.refs_5_
  33.8 0.2 shard_map.66
  34.0 0.0 collective-permute-done.8.refs_4_
  34.0 2.5 %shard_map.67 = bf16[10,384,128]{2,1,0:T(8,128)(2,1)} custom-call(bf16[10,384,128]{2,1,0:T(8,128)(2,1)S(1)} %get-tuple-element.12.refs_0_.q, bf16[16,128]{1,0:T(8,128)(2,1)S(1)} %pad.4.refs_1_, f32[10,384,256]{2,1,0:T(8,128)S(1)} %get-tuple-element.17.refs_2_, f32[10,384,128]{2,1,0:T(8,128)S(1)} %get-tuple-element.18.refs_3_, ...), custom_call_target="tpu_custom_call" | custom-call | flops 251658240 | bytes 4194304 | tf_op jit(solution)/shard_map/pallas_call | solution.py:375
  (2 shorter events, 0.0 us)
Async XLA Ops:
  1.6 16.0 %collective-permute-start.1 = (bf16[784,128]{1,0:T(8,128)(2,1)S(1)}, bf16[784,128]{1,0:T(8,128)(2,1)S(1)}, u32[]{:S(2)}, u32[]{:S(2)}) collective-permute-start(bf16[784,128]{1,0:T(8,128)(2,1)S(1)} %pad_maximum_fusion), channel_id=1, source_target_pairs={{0,4},{4,8},{8,12},{12,0},{1,5},{5,9},{9,13},{13,1},{2,6},{6,10},{... | collective-permute-start | bytes 602120 | tf_op jit(solution)/shard_map/ppermute | solution.py:29
  4.7 12.2 %collective-permute-start = (bf16[768,128]{1,0:T(8,128)(2,1)}, bf16[768,128]{1,0:T(8,128)(2,1)S(1)}, u32[]{:S(2)}, u32[]{:S(2)}) collective-permute-start(bf16[768,128]{1,0:T(8,128)(2,1)} %bitcast.15), channel_id=1, source_target_pairs={{0,4},{4,8},{8,12},{12,0},{1,5},{5,9},{9,13},{13,1},{2,6},{6,10},{... | collective-permute-start | bytes 589832 | tf_op jit(solution)/shard_map/ppermute | solution.py:29
  6.3 1.5 %collective-permute-start.2 = (bf16[256,128]{1,0:T(8,128)(2,1)}, bf16[256,128]{1,0:T(8,128)(2,1)S(1)}, u32[]{:S(2)}, u32[]{:S(2)}) collective-permute-start(bf16[256,128]{1,0:T(8,128)(2,1)} %bitcast.10), channel_id=1, source_target_pairs={{0,1},{1,0},{2,3},{3,2},{4,5},{5,4},{6,7},{7,6},{8,9},{9,8},{10,11... | collective-permute-start | bytes 196616 | tf_op jit(solution)/shard_map/ppermute | solution.py:34
  6.3 1.6 %collective-permute-start.3 = (bf16[256,128]{1,0:T(8,128)(2,1)}, bf16[256,128]{1,0:T(8,128)(2,1)S(1)}, u32[]{:S(2)}, u32[]{:S(2)}) collective-permute-start(bf16[256,128]{1,0:T(8,128)(2,1)} %bitcast.12), channel_id=1, source_target_pairs={{0,1},{1,0},{2,3},{3,2},{4,5},{5,4},{6,7},{7,6},{8,9},{9,8},{10,11... | collective-permute-start | bytes 196616 | tf_op jit(solution)/shard_map/ppermute | solution.py:34
  9.0 13.0 %collective-permute-start.4 = (bf16[512,128]{1,0:T(8,128)(2,1)S(1)}, bf16[512,128]{1,0:T(8,128)(2,1)S(1)}, u32[]{:S(2)}, u32[]{:S(2)}) collective-permute-start(bf16[512,128]{1,0:T(8,128)(2,1)S(1)} %choose.1.refs_6_), channel_id=1, source_target_pairs={{0,8},{4,12},{8,0},{12,4},{1,9},{5,13},{9,1},{13,5},{2,10},{6,14},... | collective-permute-start | bytes 393224 | tf_op jit(solution)/shard_map/ppermute | solution.py:34
  10.1 18.6 %collective-permute-start.5 = (bf16[512,128]{1,0:T(8,128)(2,1)S(1)}, bf16[512,128]{1,0:T(8,128)(2,1)S(1)}, u32[]{:S(2)}, u32[]{:S(2)}) collective-permute-start(bf16[512,128]{1,0:T(8,128)(2,1)S(1)} %choose.1.refs_6_), channel_id=1, source_target_pairs={{0,4},{4,0},{8,12},{12,8},{1,5},{5,1},{9,13},{13,9},{2,6},{6,2},{1... | collective-permute-start | bytes 393224 | tf_op jit(solution)/shard_map/ppermute | solution.py:34
  17.0 16.8 %collective-permute-start.6 = (bf16[768,128]{1,0:T(8,128)(2,1)S(1)}, bf16[768,128]{1,0:T(8,128)(2,1)S(1)}, u32[]{:S(2)}, u32[]{:S(2)}) collective-permute-start(bf16[768,128]{1,0:T(8,128)(2,1)S(1)} %collective-permute-done.refs_4_), channel_id=1, source_target_pairs={{4,8},{8,12},{5,9},{9,13},{6,10},{10,14},{7,11},{11,15},{20,24},{2... | collective-permute-start | bytes 589832 | tf_op jit(solution)/shard_map/ppermute | solution.py:29
  17.6 16.2 %collective-permute-start.7 = (bf16[784,128]{1,0:T(8,128)(2,1)S(1)}, bf16[784,128]{1,0:T(8,128)(2,1)S(1)}, u32[]{:S(2)}, u32[]{:S(2)}) collective-permute-start(bf16[784,128]{1,0:T(8,128)(2,1)S(1)} %collective-permute-done.1.refs_5_), channel_id=1, source_target_pairs={{4,8},{8,12},{5,9},{9,13},{6,10},{10,14},{7,11},{11,15},{20,24},{2... | collective-permute-start | bytes 602120 | tf_op jit(solution)/shard_map/ppermute | solution.py:29
  21.9 12.1 %collective-permute-start.8 = (bf16[512,128]{1,0:T(8,128)(2,1)S(1)}, bf16[512,128]{1,0:T(8,128)(2,1)S(1)}, u32[]{:S(2)}, u32[]{:S(2)}) collective-permute-start(bf16[512,128]{1,0:T(8,128)(2,1)S(1)} %collective-permute-done.4.refs_7_), channel_id=1, source_target_pairs={{0,4},{4,0},{8,12},{12,8},{1,5},{5,1},{9,13},{13,9},{2,6},{6,2},{1... | collective-permute-start | bytes 393224 | tf_op jit(solution)/shard_map/ppermute | solution.py:34
